TPU v7x, 32 devices: a whole 2x2x4 slice. The times are simulated.
32 devices in a mesh: box: 4 (over x, core), samp: 8 (over z, y).
Axes of the slice: x: 2, y: 2, z: 4, core: 2. Of those that a mesh axis runs over, the one named last changes fastest.
Arguments:
- child_out: float32 [1024, 2, 18432], P(('box', 'samp')), may hold values from -6 to 6
- child_octant: int32 [128, 8], P(('box', 'samp')), may hold values from 0 to 7, each once within a row
- theta_index: int32 [192, 4], replicated, may hold values from 0 to 95, as said below
- theta_weight: float32 [192, 4], replicated, may hold values from -0.2 to 0.6
- phi_index: int32 [384, 4], replicated, may hold values from 0 to 191, as said below
- phi_weight: float32 [384, 4], replicated, may hold values from -0.2 to 0.6
- shift_angle: float32 [8, 192, 384], replicated, may hold values from -3.140625 to 3.140625
- partner_src: int32 [128, 32], replicated, may hold values from 0 to 127
- partner_disp: int32 [128, 32], replicated, may hold values from 0 to 315
- translation: float32 [316, 2, 192, 384], P(None, None, 'samp'), may hold values from -0.75 to 0.75
Outputs:
- child_in: float32 [1024, 2, 18432], P(('box', 'samp'))
Inputs may be any that keep to these rules, and one draw needn't show every extreme that they name: `theta_index`: four stencil indices for each fine theta sample, consecutive coarse samples near it, clipped to the ends so that they may repeat near the poles (repeated weights add). `phi_index`: four consecutive coarse phi samples near each fine phi sample, wrapping around in phi.
All inputs are finite; a program needn't handle non-finite values.
Results may differ from a plain program's by a relative error of at most 0.00007.
Values sent between devices are 32-bit elements; how exact they have to be, the bound alone decides.
A program may use at most 256 MiB of HBM per device.

v0:
```python
import functools

import jax
import jax.numpy as jnp
from jax import lax
from jax.experimental import pallas as pl
from jax.experimental.pallas import tpu as pltpu
from jax.sharding import PartitionSpec as P

NT1 = 96
NP1 = 192
LANES = 128
MESH = pl.DeviceIdType.MESH
VMEM_LIMIT = 62 * 1024 * 1024


def split(values):
    high = values.astype(jnp.bfloat16)
    low = (values - high.astype(jnp.float32)).astype(jnp.bfloat16)
    return high, low


def dot(left, right):
    return jnp.dot(left, right, preferred_element_type=jnp.float32)


def stencil(wanted, index, weight, axis):
    total = jnp.zeros(wanted.shape, jnp.float32)
    for j in range(index.shape[axis]):
        one = slice(j, j + 1)
        spot = (slice(None), one) if axis == 1 else (one, slice(None))
        total = total + jnp.where(wanted == index[spot], weight[spot], 0.0)
    return total


def iota(shape, axis):
    return lax.broadcasted_iota(jnp.int32, shape, axis)


HALF_PI = (1.5703125, 4.837512969970703e-4, 7.54978995489188e-8)


def cos_sin(angle):
    turns = jnp.floor(angle * 0.6366197723675814 + 0.5)
    rest = ((angle - turns * HALF_PI[0]) - turns * HALF_PI[1]) - turns * HALF_PI[2]
    square = rest * rest
    sine = -1.9515295891e-4 * square + 8.3321608736e-3
    sine = (sine * square - 1.6666654611e-1) * square * rest + rest
    cosine = 2.443315711809948e-5 * square - 1.388731625493765e-3
    cosine = (cosine * square + 4.166664568298827e-2) * square * square - 0.5 * square + 1.0
    half = jnp.floor(turns * 0.5)
    odd = turns - 2.0 * half > 0.5
    flip = half - 2.0 * jnp.floor(half * 0.5) > 0.5
    sin_part = jnp.where(odd, cosine, sine)
    cos_part = jnp.where(odd, -sine, cosine)
    return jnp.where(flip, -cos_part, cos_part), jnp.where(flip, -sin_part, sin_part)


def step_kernel(
    boxes,
    samps,
    partners,
    src_rows,
    disp_rows,
    octant,
    theta_index_t,
    theta_weight_t,
    phi_index_t,
    phi_weight_t,
    child,
    angle,
    table,
    result,
    field,
    wide,
    wide_out,
    grid_sum,
    theta_up,
    theta_down,
    *scratch,
):
    half = NT1 // 2
    width = 2 * NP1
    chunks = angle.shape[2] // LANES
    rows2 = angle.shape[1]
    sources = scratch[:chunks]
    operators = scratch[chunks : 2 * chunks]
    results = scratch[2 * chunks : 3 * chunks]
    outgoing = scratch[3 * chunks : 4 * chunks]
    incoming = scratch[4 * chunks : 5 * chunks]
    cosines = scratch[5 * chunks : 6 * chunks]
    sines = scratch[6 * chunks : 7 * chunks]
    (
        child_sem,
        angle_sem,
        result_sem,
        load_sem,
        own_sem,
        out_send,
        out_recv,
        box_send,
        box_recv,
        back_own,
        back_send,
        back_recv,
    ) = scratch[7 * chunks :]
    per_device, parts = outgoing[0].shape[:2]
    kids = child.shape[0] // per_device
    per_row = width // LANES
    theta_rows = rows2 // samps
    edge = -(-(width // 2) // LANES) * LANES
    gap = edge - width // 2
    group = lax.axis_index("box")
    me = lax.axis_index("samp")
    bits = [1 << i for i in range(boxes.bit_length() - 1)][::-1]

    def mate(bit):
        return group + bit - 2 * bit * lax.rem(lax.div(group, bit), 2)

    barrier = pltpu.get_barrier_semaphore()
    for step in range(1, samps):
        pl.semaphore_signal(barrier, inc=1, device_id=(group, lax.rem(me + step, samps)), device_id_type=MESH)
    for bit in bits:
        pl.semaphore_signal(barrier, inc=1, device_id=(mate(bit), me), device_id_type=MESH)

    def load(chunk):
        return pltpu.make_async_copy(
            table.at[:, :, :, pl.ds(chunk * LANES, LANES)], operators[chunk], load_sem.at[chunk]
        )

    def keep(chunk):
        return pltpu.make_async_copy(
            outgoing[chunk].at[:, :, me], sources[chunk].at[group, me], own_sem.at[chunk]
        )

    def out_part(chunk, parent, peer):
        return pltpu.make_async_remote_copy(
            src_ref=outgoing[chunk].at[parent, :, peer],
            dst_ref=sources[chunk].at[group, me, parent],
            send_sem=out_send.at[chunk, peer],
            recv_sem=out_recv.at[chunk, me],
            device_id=(group, peer),
            device_id_type=MESH,
        )

    def out_copy(chunk, peer, owner):
        return pltpu.make_async_remote_copy(
            src_ref=outgoing[chunk].at[:, :, peer],
            dst_ref=sources[chunk].at[group, owner],
            send_sem=out_send.at[chunk, peer],
            recv_sem=out_recv.at[chunk, owner],
            device_id=(group, peer),
            device_id_type=MESH,
        )

    def back_slot(chunk, slot):
        return chunk + (slot if chunk == chunks - 1 else 0)

    def back_part(chunk, slot, peer, owner):
        return pltpu.make_async_remote_copy(
            src_ref=results[chunk].at[peer, slot],
            dst_ref=incoming[chunk].at[slot, :, owner],
            send_sem=back_send.at[chunk, peer],
            recv_sem=back_recv.at[back_slot(chunk, slot), owner],
            device_id=(group, peer),
            device_id_type=MESH,
        )

    def back_copy(chunk, peer, owner):
        return pltpu.make_async_remote_copy(
            src_ref=results[chunk].at[peer],
            dst_ref=incoming[chunk].at[:, :, owner],
            send_sem=back_send.at[chunk, peer],
            recv_sem=back_recv.at[chunk, owner],
            device_id=(group, peer),
            device_id_type=MESH,
        )

    def back_keep(chunk):
        return pltpu.make_async_copy(
            results[chunk].at[me], incoming[chunk].at[:, :, me], back_own.at[chunk]
        )

    def box_plan():
        plan = []
        held = [0]
        for bit in bits:
            plan.append((bit, list(held)))
            held = held + [h + bit for h in held]
        return plan

    plan = box_plan()

    def owner_of(mask):
        spot = group
        for bit in bits:
            if mask & bit:
                spot = spot + bit - 2 * bit * lax.rem(lax.div(group, bit), 2)
        return spot

    def hop(chunk, bit, mask):
        return pltpu.make_async_remote_copy(
            src_ref=sources[chunk].at[owner_of(mask)],
            dst_ref=sources[chunk].at[owner_of(mask)],
            send_sem=box_send.at[chunk, mask + bit],
            recv_sem=box_recv.at[chunk, mask + bit],
            device_id=(mate(bit), me),
            device_id_type=MESH,
        )

    def hop_arrival(chunk, mask):
        spot = owner_of(mask)
        return pltpu.make_async_remote_copy(
            src_ref=sources[chunk].at[spot],
            dst_ref=sources[chunk].at[spot],
            send_sem=box_send.at[chunk, mask],
            recv_sem=box_recv.at[chunk, mask],
            device_id=(mate(bits[0]), me),
            device_id_type=MESH,
        )

    def load_angle(chunk):
        return pltpu.make_async_copy(
            angle.at[:, :, pl.ds(chunk * LANES, LANES)], cosines[chunk], angle_sem.at[chunk]
        )

    load_child = pltpu.make_async_copy(child, field, child_sem)

    def tile(parent, part, place):
        return (
            pl.ds(parent * kids, kids),
            pl.ds(place * parts + part, half, stride=per_row * parts),
            slice(None),
        )

    def give(parent):
        rows = pl.ds(parent * kids, kids)
        return pltpu.make_async_copy(field.at[rows], result.at[rows], result_sem.at[parent])

    def build_theta():
        spot = iota((2 * half, rows2), 0)
        sample = jnp.where(spot < half, 2 * spot, 2 * (spot - half) + 1)
        narrow = stencil(sample, theta_index_t, theta_weight_t, 0)
        high, low = split(narrow.T)
        theta_up[:, : 2 * half] = high
        theta_up[:, 2 * half : 4 * half] = high
        theta_up[:, 4 * half :] = low
        high, low = split(narrow)
        theta_down[: 2 * half] = high
        theta_down[2 * half :] = low

    def turn(chunk):
        def one(spot, carry):
            cos_part, sin_part = cos_sin(cosines[chunk][spot])
            cosines[chunk][spot] = cos_part
            sines[chunk][spot] = sin_part
            return carry

        lax.fori_loop(0, cosines[chunk].shape[0], one, 0)

    def send_out(chunk, parent):
        def one(step, carry):
            out_part(chunk, parent, lax.rem(me + step, samps)).start()
            return carry

        lax.fori_loop(1, samps, one, 0)

    def send_last(chunk):
        send_out(chunk, per_device - 1)
        keep(chunk).start()

    def aggregate(chunk):
        lanes = slice(chunk * LANES, (chunk + 1) * LANES)
        sample = iota((edge, LANES), 0)
        mats = []
        for shift in (0, gap):
            high, low = split(stencil(sample - shift, phi_index_t[:, lanes], phi_weight_t[:, lanes], 0))
            mats.append(jnp.concatenate([high, low], axis=1))

        def one_parent(parent, carry):
            block = jnp.concatenate(
                [
                    jnp.concatenate(
                        [field[tile(parent, part, place)].reshape(kids * half, LANES) for place in range(per_row)],
                        axis=1,
                    )
                    for part in range(parts)
                ],
                axis=0,
            )
            pieces = []
            for mat, start in zip(mats, (0, width - edge)):
                high, low = split(block[:, start : start + edge])
                both = dot(high, mat)
                pieces.append(split(both[:, :LANES] + (both[:, LANES:] + dot(low, mat[:, :LANES]))))
            even, odd = pieces
            for slot, piece in enumerate((even[0], odd[0], even[1], odd[1], even[0], odd[0])):
                piece = piece.reshape(parts, kids, half, LANES)
                for part in range(parts):
                    wide[:, slot * half : (slot + 1) * half, part * LANES : (part + 1) * LANES] = piece[part]
            grid_sum[...] = jnp.zeros_like(grid_sum)

            def one_child(kid, inner):
                spot = octant[parent, kid]
                fine = dot(theta_up[...], wide[kid])
                real, imag = fine[:, :LANES], fine[:, LANES:]
                cos_part = cosines[chunk][spot]
                sin_part = sines[chunk][spot]
                grid_sum[0] += real * cos_part - imag * sin_part
                grid_sum[1] += real * sin_part + imag * cos_part
                return inner

            lax.fori_loop(0, kids, one_child, 0)
            for part in range(parts):
                for owner in range(samps):
                    outgoing[chunk][parent, part, owner] = grid_sum[
                        part, owner * theta_rows : (owner + 1) * theta_rows
                    ]

            @pl.when(parent > 0)
            def _():
                send_out(chunk, parent - 1)

            return carry

        lax.fori_loop(0, per_device, one_parent, 0)

    def disaggregate(chunk, first, last):
        rows = slice(chunk * LANES, (chunk + 1) * LANES)
        sample = iota((edge, LANES), 0)
        mats = []
        for shift in (0, gap):
            high, low = split(stencil(sample - shift, phi_index_t[:, rows], phi_weight_t[:, rows], 0).T)
            mats.append((jnp.concatenate([high, high], axis=0), low))

        def one_parent(parent, carry):
            if last:
                returned_part(chunk, parent)
            for part in range(parts):
                for owner in range(samps):
                    grid_sum[part, owner * theta_rows : (owner + 1) * theta_rows] = incoming[chunk][
                        parent, part, owner
                    ]

            def one_child(kid, inner):
                spot = octant[parent, kid]
                real, imag = grid_sum[0], grid_sum[1]
                cos_part = cosines[chunk][spot]
                sin_part = sines[chunk][spot]
                turned = jnp.concatenate(
                    [real * cos_part + imag * sin_part, imag * cos_part - real * sin_part], axis=1
                )
                high, low = split(turned)
                both = dot(theta_down[...], high)
                narrow = both[: 2 * half] + (both[2 * half :] + dot(theta_down[: 2 * half], low))
                for place, piece in enumerate(split(narrow)):
                    for parity in range(2):
                        for part in range(parts):
                            wide_out[
                                parity, kid * parts + part, :, place * LANES : (place + 1) * LANES
                            ] = piece[parity * half : (parity + 1) * half, part * LANES : (part + 1) * LANES]
                return inner

            lax.fori_loop(0, kids, one_child, 0)
            ends = []
            for parity in range(2):
                flat = wide_out[parity].reshape(kids * parts * half, 2 * LANES)
                ends.append(dot(flat, mats[parity][0]) + dot(flat[:, :LANES], mats[parity][1]))
            left, right = ends
            shared = 2 * edge - width
            joined = jnp.concatenate(
                [left[:, : edge - shared], left[:, edge - shared :] + right[:, :shared], right[:, shared:]],
                axis=1,
            ).reshape(kids, parts, half, width)
            for part in range(parts):
                for place in range(per_row):
                    spot = tile(parent, part, place)
                    piece = joined[:, part, :, place * LANES : (place + 1) * LANES]
                    if first:
                        field[spot] = piece
                    else:
                        field[spot] = field[spot] + piece
            if last:

                @pl.when(parent > 0)
                def _():
                    give(parent - 1).start()

            return carry

        lax.fori_loop(0, per_device, one_parent, 0)

    load_child.start()
    for chunk in range(chunks):
        load_angle(chunk).start()
    for chunk in range(chunks):
        load(chunk).start()
    build_theta()
    load_angle(0).wait()
    turn(0)
    load_child.wait()
    pl.semaphore_wait(barrier, samps - 1 + len(bits))
    aggregate(0)
    for chunk in range(1, chunks):
        load_angle(chunk).wait()
        turn(chunk)
        send_last(chunk - 1)
        aggregate(chunk)

    def arrive_and_share(chunk):
        def arrived(step, carry):
            peer = lax.rem(me + samps - step, samps)
            out_copy(chunk, peer, peer).wait_recv()
            return carry

        keep(chunk).wait()
        lax.fori_loop(1, samps, arrived, 0)
        for bit, held in plan:
            hop(chunk, bit, 0).start()

    def pass_on(chunk):
        for position, (bit, held) in enumerate(plan):
            for mask in held:
                if mask == 0:
                    continue
                hop(chunk, bit, mask).start()
            if position + 1 < len(plan):
                for mask in [h + bit for h in held]:
                    hop_arrival(chunk, mask).wait_recv()

    def translate(chunk):
        last_bit, last_held = plan[-1]
        for mask in [h + last_bit for h in last_held]:
            hop_arrival(chunk, mask).wait_recv()
        load(chunk).wait()

        def receivers(slot, carry):
            def one(step, inner):
                peer = lax.rem(me + 1 + step, samps)
                row = (group * samps + peer) * per_device + slot
                real = jnp.zeros(results[chunk].shape[3:], jnp.float32)
                imag = jnp.zeros(results[chunk].shape[3:], jnp.float32)
                for q in range(partners):
                    source = src_rows[q, row]
                    which = disp_rows[q, row]
                    here = lax.div(source, samps * per_device)
                    rest = lax.rem(source, samps * per_device)
                    from_samp = lax.div(rest, per_device)
                    from_slot = lax.rem(rest, per_device)
                    a = sources[chunk][here, from_samp, from_slot, 0]
                    b = sources[chunk][here, from_samp, from_slot, 1]
                    c = operators[chunk][which, 0]
                    d = operators[chunk][which, 1]
                    real = real + (c * a - d * b)
                    imag = imag + (c * b + d * a)
                results[chunk][peer, slot, 0] = real
                results[chunk][peer, slot, 1] = imag

                @pl.when(step > 0)
                def _():
                    back_part(chunk, slot, lax.rem(me + step, samps), me).start()

                return inner

            lax.fori_loop(0, samps, one, 0)
            return carry

        lax.fori_loop(0, per_device, receivers, 0)

    def returned(chunk):
        def one(step, carry):
            there = lax.rem(me + samps - step, samps)
            back_copy(chunk, there, there).wait_recv()
            return carry

        if chunk < chunks - 1:
            lax.fori_loop(1, samps, one, 0)
        back_keep(chunk).wait()

    def returned_part(chunk, parent):
        def one(step, carry):
            there = lax.rem(me + samps - step, samps)
            back_part(chunk, parent, there, there).wait_recv()
            return carry

        lax.fori_loop(1, samps, one, 0)

    send_last(chunks - 1)
    arrive_and_share(0)
    for chunk in range(chunks):
        if chunk + 1 < chunks:
            arrive_and_share(chunk + 1)
        pass_on(chunk)
        if chunk:
            back_keep(chunk - 1).start()
        translate(chunk)
    for chunk in range(chunks):
        if chunk == chunks - 1 and chunks == 1:
            back_keep(chunk).start()
        returned(chunk)
        disaggregate(chunk, chunk == 0, chunk == chunks - 1)
        if chunk == 0 and chunks > 1:
            back_keep(chunks - 1).start()
    give(per_device - 1).start()

    for chunk in range(chunks):

        def finish(step, carry, chunk=chunk):
            there = lax.rem(me + step, samps)
            out_copy(chunk, there, there).wait_send()
            back_copy(chunk, there, there).wait_send()
            return carry

        lax.fori_loop(1, samps, finish, 0)
        for bit, held in plan:
            for mask in held:
                hop(chunk, bit, mask).wait_send()
    for parent in range(per_device):
        give(parent).wait()


def local(
    boxes,
    samps,
    child_out,
    child_octant,
    theta_index,
    theta_weight,
    phi_index,
    phi_weight,
    shift_angle,
    partner_src,
    partner_disp,
    translation,
):
    child_count, parts, samples = child_out.shape
    parents, kids = child_octant.shape
    octant_count, rows2, cols2 = shift_angle.shape
    partners = partner_src.shape[1]
    theta_rows = rows2 // samps
    chunks = cols2 // LANES
    tiles = samples // LANES
    child = child_out.reshape(child_count, parts, tiles, LANES).transpose(0, 2, 1, 3)
    child = child.reshape(child_count, tiles * parts, LANES)
    block = (parents, parts, theta_rows, LANES)
    spread = (parents, parts, samps, theta_rows, LANES)
    turns = (octant_count, rows2, LANES)
    anywhere = pl.BlockSpec(memory_space=pl.ANY)
    scalars = pl.BlockSpec(memory_space=pltpu.SMEM)
    vectors = pl.BlockSpec(memory_space=pltpu.VMEM)
    dma = pltpu.SemaphoreType.DMA

    def per_chunk(shape):
        return [pltpu.VMEM(shape, jnp.float32)] * chunks

    child_in = pl.pallas_call(
        functools.partial(step_kernel, boxes, samps, partners),
        out_shape=jax.ShapeDtypeStruct(child.shape, jnp.float32),
        in_specs=[scalars] * 3 + [vectors] * 4 + [anywhere] * 3,
        out_specs=anywhere,
        scratch_shapes=[
            pltpu.VMEM(child.shape, jnp.float32),
            pltpu.VMEM((kids, 3 * NT1, parts * LANES), jnp.bfloat16),
            pltpu.VMEM((2, kids * parts, NT1 // 2, 2 * LANES), jnp.bfloat16),
            pltpu.VMEM((parts, rows2, LANES), jnp.float32),
            pltpu.VMEM((rows2, 3 * NT1), jnp.bfloat16),
            pltpu.VMEM((2 * NT1, rows2), jnp.bfloat16),
        ]
        + per_chunk((boxes, samps) + block)
        + per_chunk(translation.shape[:3] + (LANES,))
        + per_chunk((samps,) + block)
        + per_chunk(spread)
        + per_chunk(spread)
        + per_chunk(turns)
        + per_chunk(turns)
        + [
            dma(()),
            dma((chunks,)),
            dma((parents,)),
            dma((chunks,)),
            dma((chunks,)),
            dma((chunks, samps)),
            dma((chunks, samps)),
            dma((chunks, boxes)),
            dma((chunks, boxes)),
            dma((chunks,)),
            dma((chunks, samps)),
            dma((chunks - 1 + parents, samps)),
        ],
        compiler_params=pltpu.CompilerParams(
            collective_id=0, has_side_effects=True, vmem_limit_bytes=VMEM_LIMIT
        ),
    )(
        partner_src.T,
        partner_disp.T,
        child_octant,
        theta_index.T,
        theta_weight.T,
        phi_index.T,
        phi_weight.T,
        child,
        shift_angle,
        translation,
    )
    child_in = child_in.reshape(child_count, tiles, parts, LANES).transpose(0, 2, 1, 3)
    return child_in.reshape(child_count, parts, samples)


def solution(mesh):
    in_specs = (
        P(("box", "samp"), None, None),
        P(("box", "samp"), None),
        P(),
        P(),
        P(),
        P(),
        P(),
        P(),
        P(),
        P(None, None, "samp", None),
    )
    out_specs = P(("box", "samp"), None, None)
    body = functools.partial(local, mesh.shape["box"], mesh.shape["samp"])
    return jax.shard_map(body, mesh=mesh, in_specs=in_specs, out_specs=out_specs, check_vma=False)
```

profile of v0, /device:TPU:0, one launch (start us, length us, event | category | flops | bytes accessed | tf_op | source)
XLA Modules:
  0.0 140.2 jit_solution(14725695471231784147)
XLA Ops:
  0.0 135.3 %shard_map.100 = f32[32,288,128]{2,1,0:T(8,128)} custom-call(s32[32,128]{1,0:T(8,128)} %bitcast.18, s32[32,128]{1,0:T(8,128)} %bitcast.19, s32[4,8]{1,0:T(4,128)} %octant.1, s32[4,192]{1,0:T(4,128)} %bitcast.22, f32[4,192]{1,0:T(4,128)} %bitcast.23, s32[4,384]{1,0:T(4,128)} %bitcast.20, f32[4,384]{1,0:T(4,128)} %bitcast.21, f32[32,288,128]{2,1,0:T(8,128)} %bitcast.17, ...), custom_call_target="tpu_custom_call" | custom-call | tf_op jit(solution)/shard_map/pallas_call | solution.py:556
  135.3 4.8 %copy.14 = f32[32,2,18432]{2,1,0:T(2,128)} copy(f32[32,2,18432]{2,1,0:T(2,128)} %bitcast.16) | data formatting | bytes 9437184
where the time goes:
time: 141 us; the launch traced here: 140 us
  Pallas kernels  135 us (96%)
  local copies, waits for them, and re-layouts  4.84 us (3%)
    pallas_call x1, Pallas kernels, local(): pl.pallas_call(functools.partial(step_kernel, boxes, samps, partners), ou...  135 us
    unnamed x1, local copies, waits for them, and re-layouts  4.84 us

commit v1 on v0

--- a/solution.py
+++ b/solution.py
@@ -128,15 +128,21 @@
             table.at[:, :, :, pl.ds(chunk * LANES, LANES)], operators[chunk], load_sem.at[chunk]
         )
 
+    def held_by(box, samp):
+        return pl.ds((box * samps + samp) * per_device, per_device)
+
+    def held_in(box):
+        return pl.ds(box * samps * per_device, samps * per_device)
+
     def keep(chunk):
         return pltpu.make_async_copy(
-            outgoing[chunk].at[:, :, me], sources[chunk].at[group, me], own_sem.at[chunk]
+            outgoing[chunk].at[:, :, me], sources[chunk].at[held_by(group, me)], own_sem.at[chunk]
         )
 
     def out_part(chunk, parent, peer):
         return pltpu.make_async_remote_copy(
             src_ref=outgoing[chunk].at[parent, :, peer],
-            dst_ref=sources[chunk].at[group, me, parent],
+            dst_ref=sources[chunk].at[(group * samps + me) * per_device + parent],
             send_sem=out_send.at[chunk, peer],
             recv_sem=out_recv.at[chunk, me],
             device_id=(group, peer),
@@ -146,7 +152,7 @@
     def out_copy(chunk, peer, owner):
         return pltpu.make_async_remote_copy(
             src_ref=outgoing[chunk].at[:, :, peer],
-            dst_ref=sources[chunk].at[group, owner],
+            dst_ref=sources[chunk].at[held_by(group, owner)],
             send_sem=out_send.at[chunk, peer],
             recv_sem=out_recv.at[chunk, owner],
             device_id=(group, peer),
@@ -200,8 +206,8 @@
 
     def hop(chunk, bit, mask):
         return pltpu.make_async_remote_copy(
-            src_ref=sources[chunk].at[owner_of(mask)],
-            dst_ref=sources[chunk].at[owner_of(mask)],
+            src_ref=sources[chunk].at[held_in(owner_of(mask))],
+            dst_ref=sources[chunk].at[held_in(owner_of(mask))],
             send_sem=box_send.at[chunk, mask + bit],
             recv_sem=box_recv.at[chunk, mask + bit],
             device_id=(mate(bit), me),
@@ -211,8 +217,8 @@
     def hop_arrival(chunk, mask):
         spot = owner_of(mask)
         return pltpu.make_async_remote_copy(
-            src_ref=sources[chunk].at[spot],
-            dst_ref=sources[chunk].at[spot],
+            src_ref=sources[chunk].at[held_in(spot)],
+            dst_ref=sources[chunk].at[held_in(spot)],
             send_sem=box_send.at[chunk, mask],
             recv_sem=box_recv.at[chunk, mask],
             device_id=(mate(bits[0]), me),
@@ -258,9 +264,36 @@
 
         lax.fori_loop(0, cosines[chunk].shape[0], one, 0)
 
+    middle = max(1, samps // 2)
+    rim = max(1, samps // 4)
+    outer = jnp.logical_or(me < rim, me >= samps - rim)
+
+    def far(peer):
+        return lax.div(peer, middle) != lax.div(me, middle)
+
     def send_out(chunk, parent):
         def one(step, carry):
-            out_part(chunk, parent, lax.rem(me + step, samps)).start()
+            peer = lax.rem(me + step, samps)
+            if chunk == 0:
+                out_part(chunk, parent, peer).start()
+            else:
+
+                @pl.when(jnp.logical_not(jnp.logical_and(outer, far(peer))))
+                def _():
+                    out_part(chunk, parent, peer).start()
+
+            return carry
+
+        lax.fori_loop(1, samps, one, 0)
+
+    def send_far(chunk):
+        def one(step, carry):
+            peer = lax.rem(me + step, samps)
+
+            @pl.when(jnp.logical_and(outer, far(peer)))
+            def _():
+                out_copy(chunk, peer, me).start()
+
             return carry
 
         lax.fori_loop(1, samps, one, 0)
@@ -300,6 +333,10 @@
                     wide[:, slot * half : (slot + 1) * half, part * LANES : (part + 1) * LANES] = piece[part]
             grid_sum[...] = jnp.zeros_like(grid_sum)
 
+            @pl.when(parent > 0)
+            def _():
+                send_out(chunk, parent - 1)
+
             def one_child(kid, inner):
                 spot = octant[parent, kid]
                 fine = dot(theta_up[...], wide[kid])
@@ -316,11 +353,6 @@
                     outgoing[chunk][parent, part, owner] = grid_sum[
                         part, owner * theta_rows : (owner + 1) * theta_rows
                     ]
-
-            @pl.when(parent > 0)
-            def _():
-                send_out(chunk, parent - 1)
-
             return carry
 
         lax.fori_loop(0, per_device, one_parent, 0)
@@ -390,23 +422,6 @@
 
         lax.fori_loop(0, per_device, one_parent, 0)
 
-    load_child.start()
-    for chunk in range(chunks):
-        load_angle(chunk).start()
-    for chunk in range(chunks):
-        load(chunk).start()
-    build_theta()
-    load_angle(0).wait()
-    turn(0)
-    load_child.wait()
-    pl.semaphore_wait(barrier, samps - 1 + len(bits))
-    aggregate(0)
-    for chunk in range(1, chunks):
-        load_angle(chunk).wait()
-        turn(chunk)
-        send_last(chunk - 1)
-        aggregate(chunk)
-
     def arrive_and_share(chunk):
         def arrived(step, carry):
             peer = lax.rem(me + samps - step, samps)
@@ -443,12 +458,8 @@
                 for q in range(partners):
                     source = src_rows[q, row]
                     which = disp_rows[q, row]
-                    here = lax.div(source, samps * per_device)
-                    rest = lax.rem(source, samps * per_device)
-                    from_samp = lax.div(rest, per_device)
-                    from_slot = lax.rem(rest, per_device)
-                    a = sources[chunk][here, from_samp, from_slot, 0]
-                    b = sources[chunk][here, from_samp, from_slot, 1]
+                    a = sources[chunk][source, 0]
+                    b = sources[chunk][source, 1]
                     c = operators[chunk][which, 0]
                     d = operators[chunk][which, 1]
                     real = real + (c * a - d * b)
@@ -485,12 +496,39 @@
 
         lax.fori_loop(1, samps, one, 0)
 
+    load_angle(0).start()
+    load_child.start()
+    build_theta()
+    load_angle(0).wait()
+    turn(0)
+    load_child.wait()
+    for chunk in range(1, chunks):
+        load_angle(chunk).start()
+    for chunk in range(chunks):
+        load(chunk).start()
+    pl.semaphore_wait(barrier, samps - 1 + len(bits))
+    aggregate(0)
+    for chunk in range(1, chunks):
+        load_angle(chunk).wait()
+        turn(chunk)
+        send_last(chunk - 1)
+        if chunk > 1:
+            send_far(chunk - 1)
+            arrive_and_share(chunk - 2)
+        aggregate(chunk)
     send_last(chunks - 1)
-    arrive_and_share(0)
+    shared = max(0, chunks - 2)
     for chunk in range(chunks):
-        if chunk + 1 < chunks:
-            arrive_and_share(chunk + 1)
-        pass_on(chunk)
+        early = chunk < shared
+        if early:
+            pass_on(chunk)
+        if chunk == 0 and chunks > 1:
+            send_far(chunks - 1)
+        if shared < chunks:
+            arrive_and_share(shared)
+            shared += 1
+        if not early:
+            pass_on(chunk)
         if chunk:
             back_keep(chunk - 1).start()
         translate(chunk)
@@ -566,7 +604,7 @@
             pltpu.VMEM((rows2, 3 * NT1), jnp.bfloat16),
             pltpu.VMEM((2 * NT1, rows2), jnp.bfloat16),
         ]
-        + per_chunk((boxes, samps) + block)
+        + per_chunk((boxes * samps * parents,) + block[1:])
         + per_chunk(translation.shape[:3] + (LANES,))
         + per_chunk((samps,) + block)
         + per_chunk(spread)

time: 141 us -> 131 us (0.929)
  Pallas kernels: 135 us -> 125 us
    pallas_call x1, Pallas kernels: 135 us -> 125 us  [local(): pl.pallas_call(functools.partial(step_kernel, boxes, samps, partners), ou...]
where the time goes in v1:
time: 131 us; the launch traced here: 129 us
  Pallas kernels  125 us (95%)
  local copies, waits for them, and re-layouts  4.84 us (4%)
    pallas_call x1, Pallas kernels, local(): pl.pallas_call(functools.partial(step_kernel, boxes, samps, partners), ou...  125 us
    unnamed x1, local copies, waits for them, and re-layouts  4.84 us

profile of v1, /device:TPU:0, one launch (start us, length us, event | category | flops | bytes accessed | tf_op | source)
XLA Modules:
  0.0 129.5 jit_solution(9869484091954663621)
XLA Ops:
  0.0 124.6 %shard_map.100 = f32[32,288,128]{2,1,0:T(8,128)} custom-call(s32[32,128]{1,0:T(8,128)} %bitcast.18, s32[32,128]{1,0:T(8,128)} %bitcast.19, s32[4,8]{1,0:T(4,128)} %octant.1, s32[4,192]{1,0:T(4,128)} %bitcast.22, f32[4,192]{1,0:T(4,128)} %bitcast.23, s32[4,384]{1,0:T(4,128)} %bitcast.20, f32[4,384]{1,0:T(4,128)} %bitcast.21, f32[32,288,128]{2,1,0:T(8,128)} %bitcast.17, ...), custom_call_target="tpu_custom_call" | custom-call | tf_op jit(solution)/shard_map/pallas_call | solution.py:594
  124.6 4.8 %copy.14 = f32[32,2,18432]{2,1,0:T(2,128)} copy(f32[32,2,18432]{2,1,0:T(2,128)} %bitcast.16) | data formatting | bytes 9437184

commit v2 on v1

--- a/solution.py
+++ b/solution.py
@@ -11,7 +11,7 @@
 NP1 = 192
 LANES = 128
 MESH = pl.DeviceIdType.MESH
-VMEM_LIMIT = 62 * 1024 * 1024
+VMEM_LIMIT = 56 * 1024 * 1024
 
 
 def split(values):
@@ -70,7 +70,6 @@
     child,
     angle,
     table,
-    result,
     field,
     wide,
     wide_out,
@@ -93,7 +92,6 @@
     (
         child_sem,
         angle_sem,
-        result_sem,
         load_sem,
         own_sem,
         out_send,
@@ -131,8 +129,14 @@
     def held_by(box, samp):
         return pl.ds((box * samps + samp) * per_device, per_device)
 
-    def held_in(box):
-        return pl.ds(box * samps * per_device, samps * per_device)
+    middle = max(1, samps // 2)
+    side = lax.div(me, middle)
+    rim = max(1, samps // 4)
+    outer = jnp.logical_or(me < rim, me >= samps - rim)
+
+    def held_in(box, part):
+        start = side if part == 0 else 1 - side
+        return pl.ds((box * samps + start * middle) * per_device, middle * per_device)
 
     def keep(chunk):
         return pltpu.make_async_copy(
@@ -160,7 +164,7 @@
         )
 
     def back_slot(chunk, slot):
-        return chunk + (slot if chunk == chunks - 1 else 0)
+        return chunk * per_device + slot
 
     def back_part(chunk, slot, peer, owner):
         return pltpu.make_async_remote_copy(
@@ -177,7 +181,7 @@
             src_ref=results[chunk].at[peer],
             dst_ref=incoming[chunk].at[:, :, owner],
             send_sem=back_send.at[chunk, peer],
-            recv_sem=back_recv.at[chunk, owner],
+            recv_sem=back_recv.at[back_slot(chunk, 0), owner],
             device_id=(group, peer),
             device_id_type=MESH,
         )
@@ -204,23 +208,24 @@
                 spot = spot + bit - 2 * bit * lax.rem(lax.div(group, bit), 2)
         return spot
 
-    def hop(chunk, bit, mask):
+    def hop(chunk, bit, mask, part):
+        spot = held_in(owner_of(mask), part)
         return pltpu.make_async_remote_copy(
-            src_ref=sources[chunk].at[held_in(owner_of(mask))],
-            dst_ref=sources[chunk].at[held_in(owner_of(mask))],
-            send_sem=box_send.at[chunk, mask + bit],
-            recv_sem=box_recv.at[chunk, mask + bit],
+            src_ref=sources[chunk].at[spot],
+            dst_ref=sources[chunk].at[spot],
+            send_sem=box_send.at[chunk, mask + bit, part],
+            recv_sem=box_recv.at[chunk, mask + bit, part],
             device_id=(mate(bit), me),
             device_id_type=MESH,
         )
 
-    def hop_arrival(chunk, mask):
-        spot = owner_of(mask)
+    def hop_arrival(chunk, mask, part):
+        spot = held_in(owner_of(mask), part)
         return pltpu.make_async_remote_copy(
-            src_ref=sources[chunk].at[held_in(spot)],
-            dst_ref=sources[chunk].at[held_in(spot)],
-            send_sem=box_send.at[chunk, mask],
-            recv_sem=box_recv.at[chunk, mask],
+            src_ref=sources[chunk].at[spot],
+            dst_ref=sources[chunk].at[spot],
+            send_sem=box_send.at[chunk, mask, part],
+            recv_sem=box_recv.at[chunk, mask, part],
             device_id=(mate(bits[0]), me),
             device_id_type=MESH,
         )
@@ -238,10 +243,6 @@
             pl.ds(place * parts + part, half, stride=per_row * parts),
             slice(None),
         )
-
-    def give(parent):
-        rows = pl.ds(parent * kids, kids)
-        return pltpu.make_async_copy(field.at[rows], result.at[rows], result_sem.at[parent])
 
     def build_theta():
         spot = iota((2 * half, rows2), 0)
@@ -264,12 +265,8 @@
 
         lax.fori_loop(0, cosines[chunk].shape[0], one, 0)
 
-    middle = max(1, samps // 2)
-    rim = max(1, samps // 4)
-    outer = jnp.logical_or(me < rim, me >= samps - rim)
-
     def far(peer):
-        return lax.div(peer, middle) != lax.div(me, middle)
+        return lax.div(peer, middle) != side
 
     def send_out(chunk, parent):
         def one(step, carry):
@@ -302,7 +299,7 @@
         send_out(chunk, per_device - 1)
         keep(chunk).start()
 
-    def aggregate(chunk):
+    def aggregate(chunk, between):
         lanes = slice(chunk * LANES, (chunk + 1) * LANES)
         sample = iota((edge, LANES), 0)
         mats = []
@@ -333,9 +330,21 @@
                     wide[:, slot * half : (slot + 1) * half, part * LANES : (part + 1) * LANES] = piece[part]
             grid_sum[...] = jnp.zeros_like(grid_sum)
 
+            if chunk == 0:
+
+                @pl.when(parent == min(1, per_device - 1))
+                def _():
+                    pl.semaphore_wait(barrier, samps - 1 + len(bits))
+
             @pl.when(parent > 0)
             def _():
                 send_out(chunk, parent - 1)
+
+            if between:
+
+                @pl.when(parent == per_device // 2)
+                def _():
+                    run(between)
 
             def one_child(kid, inner):
                 spot = octant[parent, kid]
@@ -357,7 +366,7 @@
 
         lax.fori_loop(0, per_device, one_parent, 0)
 
-    def disaggregate(chunk, first, last):
+    def disaggregate(chunk, first):
         rows = slice(chunk * LANES, (chunk + 1) * LANES)
         sample = iota((edge, LANES), 0)
         mats = []
@@ -366,8 +375,7 @@
             mats.append((jnp.concatenate([high, high], axis=0), low))
 
         def one_parent(parent, carry):
-            if last:
-                returned_part(chunk, parent)
+            returned_part(chunk, parent)
             for part in range(parts):
                 for owner in range(samps):
                     grid_sum[part, owner * theta_rows : (owner + 1) * theta_rows] = incoming[chunk][
@@ -412,44 +420,64 @@
                         field[spot] = piece
                     else:
                         field[spot] = field[spot] + piece
-            if last:
-
-                @pl.when(parent > 0)
-                def _():
-                    give(parent - 1).start()
-
             return carry
 
         lax.fori_loop(0, per_device, one_parent, 0)
 
-    def arrive_and_share(chunk):
-        def arrived(step, carry):
-            peer = lax.rem(me + samps - step, samps)
+    def share(chunk, part):
+        def near_one(step, carry):
+            peer = side * middle + lax.rem(me - side * middle + step, middle)
             out_copy(chunk, peer, peer).wait_recv()
             return carry
 
-        keep(chunk).wait()
-        lax.fori_loop(1, samps, arrived, 0)
+        def far_one(step, carry):
+            peer = (1 - side) * middle + step
+            out_copy(chunk, peer, peer).wait_recv()
+            return carry
+
+        if part == 0:
+            keep(chunk).wait()
+            lax.fori_loop(1, middle, near_one, 0)
+        else:
+            lax.fori_loop(0, middle, far_one, 0)
         for bit, held in plan:
-            hop(chunk, bit, 0).start()
-
-    def pass_on(chunk):
+            hop(chunk, bit, 0, part).start()
+
+    def pass_on(chunk, part):
         for position, (bit, held) in enumerate(plan):
             for mask in held:
                 if mask == 0:
                     continue
-                hop(chunk, bit, mask).start()
+                hop(chunk, bit, mask, part).start()
             if position + 1 < len(plan):
                 for mask in [h + bit for h in held]:
-                    hop_arrival(chunk, mask).wait_recv()
-
-    def translate(chunk):
+                    hop_arrival(chunk, mask, part).wait_recv()
+
+    def back_far(chunk):
+        def one(spot, carry):
+            slot = lax.div(spot, middle)
+            peer = (1 - side) * middle + lax.rem(spot, middle)
+            back_part(chunk, slot, peer, me).start()
+            return carry
+
+        @pl.when(outer)
+        def _():
+            lax.fori_loop(0, per_device * middle, one, 0)
+
+    def translate(chunk, between):
         last_bit, last_held = plan[-1]
         for mask in [h + last_bit for h in last_held]:
-            hop_arrival(chunk, mask).wait_recv()
+            for part in range(2):
+                hop_arrival(chunk, mask, part).wait_recv()
         load(chunk).wait()
 
         def receivers(slot, carry):
+            if between:
+
+                @pl.when(slot == per_device // 2)
+                def _():
+                    run(between)
+
             def one(step, inner):
                 peer = lax.rem(me + 1 + step, samps)
                 row = (group * samps + peer) * per_device + slot
@@ -467,9 +495,11 @@
                 results[chunk][peer, slot, 0] = real
                 results[chunk][peer, slot, 1] = imag
 
-                @pl.when(step > 0)
+                there = lax.rem(me + step, samps)
+
+                @pl.when(jnp.logical_and(step > 0, jnp.logical_not(jnp.logical_and(outer, far(there)))))
                 def _():
-                    back_part(chunk, slot, lax.rem(me + step, samps), me).start()
+                    back_part(chunk, slot, there, me).start()
 
                 return inner
 
@@ -477,16 +507,6 @@
             return carry
 
         lax.fori_loop(0, per_device, receivers, 0)
-
-    def returned(chunk):
-        def one(step, carry):
-            there = lax.rem(me + samps - step, samps)
-            back_copy(chunk, there, there).wait_recv()
-            return carry
-
-        if chunk < chunks - 1:
-            lax.fori_loop(1, samps, one, 0)
-        back_keep(chunk).wait()
 
     def returned_part(chunk, parent):
         def one(step, carry):
@@ -506,55 +526,76 @@
         load_angle(chunk).start()
     for chunk in range(chunks):
         load(chunk).start()
-    pl.semaphore_wait(barrier, samps - 1 + len(bits))
-    aggregate(0)
+    called = set()
+
+    def fresh(*calls):
+        left = [call for call in calls if 0 <= call[1] < chunks and call not in called]
+        called.update(left)
+        return left
+
+    def run(calls):
+        for function, *rest in calls:
+            function(*rest)
+
+    aggregate(0, [])
     for chunk in range(1, chunks):
         load_angle(chunk).wait()
         turn(chunk)
         send_last(chunk - 1)
         if chunk > 1:
-            send_far(chunk - 1)
-            arrive_and_share(chunk - 2)
-        aggregate(chunk)
-    send_last(chunks - 1)
-    shared = max(0, chunks - 2)
+            run(fresh((send_far, chunk - 1)))
+        run(fresh((share, chunk - 2, 1)))
+        aggregate(chunk, fresh((share, chunk - 1, 0), (pass_on, chunk - 2, 0)))
+    last = chunks - 1
+    send_last(last)
     for chunk in range(chunks):
-        early = chunk < shared
-        if early:
-            pass_on(chunk)
+        if chunk == last:
+            run(fresh((pass_on, last, 0), (share, last, 1), (back_far, last - 2)))
+        run(fresh((share, chunk, 0), (pass_on, chunk, 0)))
         if chunk == 0 and chunks > 1:
-            send_far(chunks - 1)
-        if shared < chunks:
-            arrive_and_share(shared)
-            shared += 1
-        if not early:
-            pass_on(chunk)
+            run(fresh((pass_on, 0, 1)) if chunks > 2 else [])
+            run(fresh((send_far, last)))
+        run(fresh((share, chunk, 1), (pass_on, chunk, 1)))
         if chunk:
             back_keep(chunk - 1).start()
-        translate(chunk)
-    for chunk in range(chunks):
-        if chunk == chunks - 1 and chunks == 1:
-            back_keep(chunk).start()
-        returned(chunk)
-        disaggregate(chunk, chunk == 0, chunk == chunks - 1)
-        if chunk == 0 and chunks > 1:
-            back_keep(chunks - 1).start()
-    give(per_device - 1).start()
+        translate(chunk, fresh((share, chunk + 1, 1), (share, last, 0)) if chunk + 1 < last else [])
+    for chunk in range(last):
+        run(fresh((back_far, chunk)))
+        if chunk + 1 < last:
+            run(fresh((back_far, chunk + 1)))
+        back_keep(chunk).wait()
+        if chunk + 1 == last:
+            run(fresh((back_far, last)))
+        if chunk == 0:
+            back_keep(last).start()
+        disaggregate(chunk, chunk == 0)
+    if last == 0:
+        run(fresh((back_far, last)))
+        back_keep(last).start()
+    back_keep(last).wait()
 
     for chunk in range(chunks):
 
         def finish(step, carry, chunk=chunk):
             there = lax.rem(me + step, samps)
             out_copy(chunk, there, there).wait_send()
-            back_copy(chunk, there, there).wait_send()
+            if chunk < last:
+                back_copy(chunk, there, there).wait_send()
             return carry
 
         lax.fori_loop(1, samps, finish, 0)
         for bit, held in plan:
             for mask in held:
-                hop(chunk, bit, mask).wait_send()
-    for parent in range(per_device):
-        give(parent).wait()
+                for part in range(2):
+                    hop(chunk, bit, mask, part).wait_send()
+    disaggregate(last, last == 0)
+
+    def finish_last(step, carry):
+        there = lax.rem(me + step, samps)
+        back_copy(last, there, there).wait_send()
+        return carry
+
+    lax.fori_loop(1, samps, finish_last, 0)
 
 
 def local(
@@ -593,11 +634,10 @@
 
     child_in = pl.pallas_call(
         functools.partial(step_kernel, boxes, samps, partners),
-        out_shape=jax.ShapeDtypeStruct(child.shape, jnp.float32),
+        out_shape=pltpu.VMEM(child.shape, jnp.float32),
         in_specs=[scalars] * 3 + [vectors] * 4 + [anywhere] * 3,
-        out_specs=anywhere,
+        out_specs=vectors,
         scratch_shapes=[
-            pltpu.VMEM(child.shape, jnp.float32),
             pltpu.VMEM((kids, 3 * NT1, parts * LANES), jnp.bfloat16),
             pltpu.VMEM((2, kids * parts, NT1 // 2, 2 * LANES), jnp.bfloat16),
             pltpu.VMEM((parts, rows2, LANES), jnp.float32),
@@ -614,16 +654,15 @@
         + [
             dma(()),
             dma((chunks,)),
-            dma((parents,)),
             dma((chunks,)),
             dma((chunks,)),
             dma((chunks, samps)),
             dma((chunks, samps)),
-            dma((chunks, boxes)),
-            dma((chunks, boxes)),
+            dma((chunks, boxes, 2)),
+            dma((chunks, boxes, 2)),
             dma((chunks,)),
             dma((chunks, samps)),
-            dma((chunks - 1 + parents, samps)),
+            dma((chunks * parents, samps)),
         ],
         compiler_params=pltpu.CompilerParams(
             collective_id=0, has_side_effects=True, vmem_limit_bytes=VMEM_LIMIT

time: 131 us -> 121 us (0.924)
  Pallas kernels: 125 us -> 118 us
  local copies, waits for them, and re-layouts: 4.84 us -> 2.19 us
    pallas_call x1, Pallas kernels: 125 us -> 118 us  [local(): pl.pallas_call(functools.partial(step_kernel, boxes, samps, partners), ou...]
    unnamed x1, local copies, waits for them, and re-layouts: 4.84 us -> 2.19 us
where the time goes in v2:
time: 121 us; the launch traced here: 120 us
  Pallas kernels  118 us (98%)
  local copies, waits for them, and re-layouts  2.19 us (2%)
    pallas_call x1, Pallas kernels, local(): pl.pallas_call(functools.partial(step_kernel, boxes, samps, partners), ou...  118 us

profile of v2, /device:TPU:0, one launch (start us, length us, event | category | flops | bytes accessed | tf_op | source)
XLA Modules:
  0.0 119.8 jit_solution(10826238488405076951)
XLA Ops:
  0.0 117.6 %shard_map.100 = f32[32,288,128]{2,1,0:T(8,128)S(1)} custom-call(s32[32,128]{1,0:T(8,128)} %bitcast.18, s32[32,128]{1,0:T(8,128)} %bitcast.19, s32[4,8]{1,0:T(4,128)} %octant.1, s32[4,192]{1,0:T(4,128)} %bitcast.22, f32[4,192]{1,0:T(4,128)} %bitcast.23, s32[4,384]{1,0:T(4,128)} %bitcast.20, f32[4,384]{1,0:T(4,128)} %bitcast.21, f32[32,288,128]{2,1,0:T(8,128)} %bitcast.17, ...), custom_call_target="tpu_custom_call" | custom-call | tf_op jit(solution)/shard_map/pallas_call | solution.py:635
  117.6 2.2 %copy.14 = f32[32,2,18432]{2,1,0:T(2,128)} copy(f32[32,2,18432]{2,1,0:T(2,128)S(1)} %bitcast.16) | data formatting | bytes 9437184

commit v3 on v2

--- a/solution.py
+++ b/solution.py
@@ -60,13 +60,13 @@
     boxes,
     samps,
     partners,
-    src_rows,
-    disp_rows,
-    octant,
-    theta_index_t,
-    theta_weight_t,
-    phi_index_t,
-    phi_weight_t,
+    src_in,
+    disp_in,
+    octant_in,
+    theta_index_in,
+    theta_weight_in,
+    phi_index_in,
+    phi_weight_in,
     child,
     angle,
     table,
@@ -76,6 +76,13 @@
     grid_sum,
     theta_up,
     theta_down,
+    src_rows,
+    disp_rows,
+    octant,
+    theta_index_t,
+    theta_weight_t,
+    phi_index_t,
+    phi_weight_t,
     *scratch,
 ):
     half = NT1 // 2
@@ -93,7 +100,6 @@
         child_sem,
         angle_sem,
         load_sem,
-        own_sem,
         out_send,
         out_recv,
         box_send,
@@ -101,6 +107,7 @@
         back_own,
         back_send,
         back_recv,
+        small_sem,
     ) = scratch[7 * chunks :]
     per_device, parts = outgoing[0].shape[:2]
     kids = child.shape[0] // per_device
@@ -134,57 +141,50 @@
     rim = max(1, samps // 4)
     outer = jnp.logical_or(me < rim, me >= samps - rim)
 
+    def apart(peer):
+        return lax.rem(lax.div(peer, middle) + side, 2)
+
     def held_in(box, part):
         start = side if part == 0 else 1 - side
         return pl.ds((box * samps + start * middle) * per_device, middle * per_device)
 
     def keep(chunk):
         return pltpu.make_async_copy(
-            outgoing[chunk].at[:, :, me], sources[chunk].at[held_by(group, me)], own_sem.at[chunk]
+            outgoing[chunk].at[:, :, me], sources[chunk].at[held_by(group, me)], out_recv.at[chunk, 0]
         )
 
     def out_part(chunk, parent, peer):
         return pltpu.make_async_remote_copy(
             src_ref=outgoing[chunk].at[parent, :, peer],
             dst_ref=sources[chunk].at[(group * samps + me) * per_device + parent],
-            send_sem=out_send.at[chunk, peer],
-            recv_sem=out_recv.at[chunk, me],
+            send_sem=out_send.at[chunk],
+            recv_sem=out_recv.at[chunk, apart(peer)],
             device_id=(group, peer),
             device_id_type=MESH,
         )
 
-    def out_copy(chunk, peer, owner):
+    def out_copy(chunk, peer):
         return pltpu.make_async_remote_copy(
             src_ref=outgoing[chunk].at[:, :, peer],
-            dst_ref=sources[chunk].at[held_by(group, owner)],
-            send_sem=out_send.at[chunk, peer],
-            recv_sem=out_recv.at[chunk, owner],
+            dst_ref=sources[chunk].at[held_by(group, me)],
+            send_sem=out_send.at[chunk],
+            recv_sem=out_recv.at[chunk, apart(peer)],
             device_id=(group, peer),
             device_id_type=MESH,
         )
 
-    def back_slot(chunk, slot):
-        return chunk * per_device + slot
-
-    def back_part(chunk, slot, peer, owner):
+    def back_part(chunk, slot, peer):
         return pltpu.make_async_remote_copy(
             src_ref=results[chunk].at[peer, slot],
-            dst_ref=incoming[chunk].at[slot, :, owner],
-            send_sem=back_send.at[chunk, peer],
-            recv_sem=back_recv.at[back_slot(chunk, slot), owner],
+            dst_ref=incoming[chunk].at[slot, :, me],
+            send_sem=back_send.at[chunk],
+            recv_sem=back_recv.at[chunk * per_device + slot],
             device_id=(group, peer),
             device_id_type=MESH,
         )
 
-    def back_copy(chunk, peer, owner):
-        return pltpu.make_async_remote_copy(
-            src_ref=results[chunk].at[peer],
-            dst_ref=incoming[chunk].at[:, :, owner],
-            send_sem=back_send.at[chunk, peer],
-            recv_sem=back_recv.at[back_slot(chunk, 0), owner],
-            device_id=(group, peer),
-            device_id_type=MESH,
-        )
+    def await_bytes(ref, sem):
+        pltpu.make_async_copy(ref, ref, sem).wait()
 
     def back_keep(chunk):
         return pltpu.make_async_copy(
@@ -208,25 +208,17 @@
                 spot = spot + bit - 2 * bit * lax.rem(lax.div(group, bit), 2)
         return spot
 
+    def hop_slot(mask, part):
+        return 0 if mask % 2 else mask - 1 + part
+
     def hop(chunk, bit, mask, part):
         spot = held_in(owner_of(mask), part)
         return pltpu.make_async_remote_copy(
             src_ref=sources[chunk].at[spot],
             dst_ref=sources[chunk].at[spot],
-            send_sem=box_send.at[chunk, mask + bit, part],
-            recv_sem=box_recv.at[chunk, mask + bit, part],
+            send_sem=box_send.at[chunk],
+            recv_sem=box_recv.at[chunk, hop_slot(mask + bit, part)],
             device_id=(mate(bit), me),
-            device_id_type=MESH,
-        )
-
-    def hop_arrival(chunk, mask, part):
-        spot = held_in(owner_of(mask), part)
-        return pltpu.make_async_remote_copy(
-            src_ref=sources[chunk].at[spot],
-            dst_ref=sources[chunk].at[spot],
-            send_sem=box_send.at[chunk, mask, part],
-            recv_sem=box_recv.at[chunk, mask, part],
-            device_id=(mate(bits[0]), me),
             device_id_type=MESH,
         )
 
@@ -235,7 +227,23 @@
             angle.at[:, :, pl.ds(chunk * LANES, LANES)], cosines[chunk], angle_sem.at[chunk]
         )
 
-    load_child = pltpu.make_async_copy(child, field, child_sem)
+    small = [
+        pltpu.make_async_copy(source, place, small_sem.at[spot])
+        for spot, (source, place) in enumerate(
+            (
+                (octant_in, octant),
+                (theta_index_in, theta_index_t),
+                (theta_weight_in, theta_weight_t),
+                (phi_index_in, phi_index_t),
+                (phi_weight_in, phi_weight_t),
+                (src_in, src_rows),
+                (disp_in, disp_rows),
+            )
+        )
+    ]
+    def load_child(parent):
+        rows = pl.ds(parent * kids, kids)
+        return pltpu.make_async_copy(child.at[rows], field.at[rows], child_sem.at[parent])
 
     def tile(parent, part, place):
         return (
@@ -289,14 +297,15 @@
 
             @pl.when(jnp.logical_and(outer, far(peer)))
             def _():
-                out_copy(chunk, peer, me).start()
+                out_copy(chunk, peer).start()
 
             return carry
 
         lax.fori_loop(1, samps, one, 0)
 
     def send_last(chunk):
-        send_out(chunk, per_device - 1)
+        if chunk > 0:
+            send_out(chunk, per_device - 1)
         keep(chunk).start()
 
     def aggregate(chunk, between):
@@ -330,15 +339,11 @@
                     wide[:, slot * half : (slot + 1) * half, part * LANES : (part + 1) * LANES] = piece[part]
             grid_sum[...] = jnp.zeros_like(grid_sum)
 
-            if chunk == 0:
-
-                @pl.when(parent == min(1, per_device - 1))
+            if chunk > 0:
+
+                @pl.when(parent > 0)
                 def _():
-                    pl.semaphore_wait(barrier, samps - 1 + len(bits))
-
-            @pl.when(parent > 0)
-            def _():
-                send_out(chunk, parent - 1)
+                    send_out(chunk, parent - 1)
 
             if between:
 
@@ -362,11 +367,18 @@
                     outgoing[chunk][parent, part, owner] = grid_sum[
                         part, owner * theta_rows : (owner + 1) * theta_rows
                     ]
+            if chunk == 0:
+
+                @pl.when(parent == 0)
+                def _():
+                    pl.semaphore_wait(barrier, samps - 1 + len(bits))
+
+                send_out(chunk, parent)
             return carry
 
         lax.fori_loop(0, per_device, one_parent, 0)
 
-    def disaggregate(chunk, first):
+    def disaggregate(chunk, first, between):
         rows = slice(chunk * LANES, (chunk + 1) * LANES)
         sample = iota((edge, LANES), 0)
         mats = []
@@ -376,6 +388,8 @@
 
         def one_parent(parent, carry):
             returned_part(chunk, parent)
+            for function, *rest in between:
+                function(*rest, parent)
             for part in range(parts):
                 for owner in range(samps):
                     grid_sum[part, owner * theta_rows : (owner + 1) * theta_rows] = incoming[chunk][
@@ -425,21 +439,7 @@
         lax.fori_loop(0, per_device, one_parent, 0)
 
     def share(chunk, part):
-        def near_one(step, carry):
-            peer = side * middle + lax.rem(me - side * middle + step, middle)
-            out_copy(chunk, peer, peer).wait_recv()
-            return carry
-
-        def far_one(step, carry):
-            peer = (1 - side) * middle + step
-            out_copy(chunk, peer, peer).wait_recv()
-            return carry
-
-        if part == 0:
-            keep(chunk).wait()
-            lax.fori_loop(1, middle, near_one, 0)
-        else:
-            lax.fori_loop(0, middle, far_one, 0)
+        await_bytes(sources[chunk].at[held_in(group, part)], out_recv.at[chunk, part])
         for bit, held in plan:
             hop(chunk, bit, 0, part).start()
 
@@ -451,24 +451,26 @@
                 hop(chunk, bit, mask, part).start()
             if position + 1 < len(plan):
                 for mask in [h + bit for h in held]:
-                    hop_arrival(chunk, mask, part).wait_recv()
-
-    def back_far(chunk):
-        def one(spot, carry):
-            slot = lax.div(spot, middle)
-            peer = (1 - side) * middle + lax.rem(spot, middle)
-            back_part(chunk, slot, peer, me).start()
+                    await_bytes(sources[chunk].at[held_in(owner_of(mask), part)], box_recv.at[chunk, hop_slot(mask, part)])
+
+    def back_far_part(chunk, slot):
+        def one(step, carry):
+            back_part(chunk, slot, (1 - side) * middle + step).start()
             return carry
 
         @pl.when(outer)
         def _():
-            lax.fori_loop(0, per_device * middle, one, 0)
+            lax.fori_loop(0, middle, one, 0)
+
+    def back_far(chunk):
+        def one(slot, carry):
+            back_far_part(chunk, slot)
+            return carry
+
+        lax.fori_loop(0, per_device, one, 0)
 
     def translate(chunk, between):
-        last_bit, last_held = plan[-1]
-        for mask in [h + last_bit for h in last_held]:
-            for part in range(2):
-                hop_arrival(chunk, mask, part).wait_recv()
+        await_bytes(sources[chunk].at[pl.ds(0, boxes // 2 * samps * per_device)], box_recv.at[chunk, 0])
         load(chunk).wait()
 
         def receivers(slot, carry):
@@ -499,7 +501,7 @@
 
                 @pl.when(jnp.logical_and(step > 0, jnp.logical_not(jnp.logical_and(outer, far(there)))))
                 def _():
-                    back_part(chunk, slot, there, me).start()
+                    back_part(chunk, slot, there).start()
 
                 return inner
 
@@ -509,24 +511,25 @@
         lax.fori_loop(0, per_device, receivers, 0)
 
     def returned_part(chunk, parent):
-        def one(step, carry):
-            there = lax.rem(me + samps - step, samps)
-            back_part(chunk, parent, there, there).wait_recv()
-            return carry
-
-        lax.fori_loop(1, samps, one, 0)
+        await_bytes(incoming[chunk].at[parent, :, pl.ds(0, samps - 1)], back_recv.at[chunk * per_device + parent])
 
     load_angle(0).start()
-    load_child.start()
-    build_theta()
+    for parent in range(per_device):
+        load_child(parent).start()
+    for copy in small:
+        copy.start()
     load_angle(0).wait()
     turn(0)
-    load_child.wait()
+    for copy in small:
+        copy.wait()
+    build_theta()
+    for parent in range(per_device):
+        load_child(parent).wait()
     for chunk in range(1, chunks):
         load_angle(chunk).start()
     for chunk in range(chunks):
         load(chunk).start()
-    called = set()
+    called = {(send_far, 0)}
 
     def fresh(*calls):
         left = [call for call in calls if 0 <= call[1] < chunks and call not in called]
@@ -550,52 +553,32 @@
     send_last(last)
     for chunk in range(chunks):
         if chunk == last:
-            run(fresh((pass_on, last, 0), (share, last, 1), (back_far, last - 2)))
+            run(fresh((send_far, last), (pass_on, last, 0), (share, last, 1), (back_far, last - 2)))
         run(fresh((share, chunk, 0), (pass_on, chunk, 0)))
-        if chunk == 0 and chunks > 1:
-            run(fresh((pass_on, 0, 1)) if chunks > 2 else [])
-            run(fresh((send_far, last)))
         run(fresh((share, chunk, 1), (pass_on, chunk, 1)))
         if chunk:
             back_keep(chunk - 1).start()
-        translate(chunk, fresh((share, chunk + 1, 1), (share, last, 0)) if chunk + 1 < last else [])
+        translate(chunk, fresh((share, chunk + 1, 1), (send_far, last), (share, last, 0)) if chunk + 1 < last else [])
     for chunk in range(last):
         run(fresh((back_far, chunk)))
         if chunk + 1 < last:
             run(fresh((back_far, chunk + 1)))
         back_keep(chunk).wait()
-        if chunk + 1 == last:
-            run(fresh((back_far, last)))
         if chunk == 0:
             back_keep(last).start()
-        disaggregate(chunk, chunk == 0)
+        disaggregate(chunk, chunk == 0, [(back_far_part, last)] if chunk + 1 == last else [])
     if last == 0:
         run(fresh((back_far, last)))
         back_keep(last).start()
     back_keep(last).wait()
 
     for chunk in range(chunks):
-
-        def finish(step, carry, chunk=chunk):
-            there = lax.rem(me + step, samps)
-            out_copy(chunk, there, there).wait_send()
-            if chunk < last:
-                back_copy(chunk, there, there).wait_send()
-            return carry
-
-        lax.fori_loop(1, samps, finish, 0)
-        for bit, held in plan:
-            for mask in held:
-                for part in range(2):
-                    hop(chunk, bit, mask, part).wait_send()
-    disaggregate(last, last == 0)
-
-    def finish_last(step, carry):
-        there = lax.rem(me + step, samps)
-        back_copy(last, there, there).wait_send()
-        return carry
-
-    lax.fori_loop(1, samps, finish_last, 0)
+        await_bytes(outgoing[chunk].at[:, :, pl.ds(0, samps - 1)], out_send.at[chunk])
+        await_bytes(sources[chunk].at[pl.ds(0, (boxes - 1) * samps * per_device)], box_send.at[chunk])
+        if chunk < last:
+            await_bytes(results[chunk].at[pl.ds(0, samps - 1)], back_send.at[chunk])
+    disaggregate(last, last == 0, [])
+    await_bytes(results[last].at[pl.ds(0, samps - 1)], back_send.at[last])
 
 
 def local(
@@ -625,7 +608,6 @@
     spread = (parents, parts, samps, theta_rows, LANES)
     turns = (octant_count, rows2, LANES)
     anywhere = pl.BlockSpec(memory_space=pl.ANY)
-    scalars = pl.BlockSpec(memory_space=pltpu.SMEM)
     vectors = pl.BlockSpec(memory_space=pltpu.VMEM)
     dma = pltpu.SemaphoreType.DMA
 
@@ -635,7 +617,7 @@
     child_in = pl.pallas_call(
         functools.partial(step_kernel, boxes, samps, partners),
         out_shape=pltpu.VMEM(child.shape, jnp.float32),
-        in_specs=[scalars] * 3 + [vectors] * 4 + [anywhere] * 3,
+        in_specs=[anywhere] * 10,
         out_specs=vectors,
         scratch_shapes=[
             pltpu.VMEM((kids, 3 * NT1, parts * LANES), jnp.bfloat16),
@@ -643,6 +625,13 @@
             pltpu.VMEM((parts, rows2, LANES), jnp.float32),
             pltpu.VMEM((rows2, 3 * NT1), jnp.bfloat16),
             pltpu.VMEM((2 * NT1, rows2), jnp.bfloat16),
+            pltpu.SMEM(partner_src.shape[::-1], jnp.int32),
+            pltpu.SMEM(partner_disp.shape[::-1], jnp.int32),
+            pltpu.SMEM(child_octant.shape, jnp.int32),
+            pltpu.VMEM(theta_index.shape[::-1], jnp.int32),
+            pltpu.VMEM(theta_weight.shape[::-1], jnp.float32),
+            pltpu.VMEM(phi_index.shape[::-1], jnp.int32),
+            pltpu.VMEM(phi_weight.shape[::-1], jnp.float32),
         ]
         + per_chunk((boxes * samps * parents,) + block[1:])
         + per_chunk(translation.shape[:3] + (LANES,))
@@ -652,17 +641,17 @@
         + per_chunk(turns)
         + per_chunk(turns)
         + [
-            dma(()),
+            dma((parents,)),
             dma((chunks,)),
             dma((chunks,)),
             dma((chunks,)),
-            dma((chunks, samps)),
-            dma((chunks, samps)),
-            dma((chunks, boxes, 2)),
-            dma((chunks, boxes, 2)),
+            dma((chunks, 2)),
             dma((chunks,)),
-            dma((chunks, samps)),
-            dma((chunks * parents, samps)),
+            dma((chunks, boxes - 1)),
+            dma((chunks,)),
+            dma((chunks,)),
+            dma((chunks * parents,)),
+            dma((7,)),
         ],
         compiler_params=pltpu.CompilerParams(
             collective_id=0, has_side_effects=True, vmem_limit_bytes=VMEM_LIMIT

time: 121 us -> 118 us (0.975)
  Pallas kernels: 118 us -> 115 us
    pallas_call x1, Pallas kernels: 118 us -> 115 us  [local(): pl.pallas_call(functools.partial(step_kernel, boxes, samps, partners), ou...]
where the time goes in v3:
time: 118 us
  Pallas kernels  115 us (97%)
  local copies, waits for them, and re-layouts  2.19 us (2%)
    pallas_call x1, Pallas kernels, local(): pl.pallas_call(functools.partial(step_kernel, boxes, samps, partners), ou...  115 us

profile of v3, /device:TPU:0, one launch (start us, length us, event | category | flops | bytes accessed | tf_op | source)
XLA Modules:
  0.0 117.6 jit_solution(3027606922847049)
XLA Ops:
  0.0 115.4 %shard_map.100 = f32[32,288,128]{2,1,0:T(8,128)S(1)} custom-call(s32[32,128]{1,0:T(8,128)} %bitcast.18, s32[32,128]{1,0:T(8,128)} %bitcast.19, s32[4,8]{1,0:T(4,128)} %octant_in.1, s32[4,192]{1,0:T(4,128)} %bitcast.22, f32[4,192]{1,0:T(4,128)} %bitcast.23, s32[4,384]{1,0:T(4,128)} %bitcast.20, f32[4,384]{1,0:T(4,128)} %bitcast.21, f32[32,288,128]{2,1,0:T(8,128)} %bitcast.17, ...), custom_call_target="tpu_custom_call" | custom-call | tf_op jit(solution)/shard_map/pallas_call | solution.py:617
  115.4 2.2 %copy.14 = f32[32,2,18432]{2,1,0:T(2,128)} copy(f32[32,2,18432]{2,1,0:T(2,128)S(1)} %bitcast.16) | data formatting | bytes 9437184

commit v4 on v3

--- a/solution.py
+++ b/solution.py
@@ -11,6 +11,7 @@
 NP1 = 192
 LANES = 128
 MESH = pl.DeviceIdType.MESH
+DELAY = 1
 VMEM_LIMIT = 56 * 1024 * 1024
 
 
@@ -136,10 +137,15 @@
     def held_by(box, samp):
         return pl.ds((box * samps + samp) * per_device, per_device)
 
+    last = chunks - 1
     middle = max(1, samps // 2)
     side = lax.div(me, middle)
     rim = max(1, samps // 4)
-    outer = jnp.logical_or(me < rim, me >= samps - rim)
+
+    def at_rim(peer):
+        return jnp.logical_or(peer < rim, peer >= samps - rim)
+
+    outer = at_rim(me)
 
     def apart(peer):
         return lax.rem(lax.div(peer, middle) + side, 2)
@@ -277,19 +283,24 @@
         return lax.div(peer, middle) != side
 
     def send_out(chunk, parent):
-        def one(step, carry):
-            peer = lax.rem(me + step, samps)
-            if chunk == 0:
-                out_part(chunk, parent, peer).start()
-            else:
-
-                @pl.when(jnp.logical_not(jnp.logical_and(outer, far(peer))))
-                def _():
-                    out_part(chunk, parent, peer).start()
-
-            return carry
-
-        lax.fori_loop(1, samps, one, 0)
+        spot = me - side * middle
+
+        def near_one(step, carry):
+            out_part(chunk, parent, side * middle + lax.rem(spot + step, middle)).start()
+            return carry
+
+        def far_one(step, carry):
+            out_part(chunk, parent, (1 - side) * middle + lax.rem(spot + step, middle)).start()
+            return carry
+
+        lax.fori_loop(1, middle, near_one, 0)
+        if chunk == 0:
+            lax.fori_loop(0, middle, far_one, 0)
+        else:
+
+            @pl.when(jnp.logical_not(outer))
+            def _():
+                lax.fori_loop(0, middle, far_one, 0)
 
     def send_far(chunk):
         def one(step, carry):
@@ -316,7 +327,9 @@
             high, low = split(stencil(sample - shift, phi_index_t[:, lanes], phi_weight_t[:, lanes], 0))
             mats.append(jnp.concatenate([high, low], axis=1))
 
-        def one_parent(parent, carry):
+        def interpolate(parent):
+            if chunk == 0:
+                load_child(parent).wait()
             block = jnp.concatenate(
                 [
                     jnp.concatenate(
@@ -337,6 +350,52 @@
                 piece = piece.reshape(parts, kids, half, LANES)
                 for part in range(parts):
                     wide[:, slot * half : (slot + 1) * half, part * LANES : (part + 1) * LANES] = piece[part]
+
+        def first_half(turned, carry):
+            part_of = lax.rem(turned + 1 - side, 2)
+            rows = pl.ds(pl.multiple_of(part_of * (rows2 // 2), rows2 // 2), rows2 // 2)
+
+            def one_octant(spot, inner):
+                kid = 0
+                for other in range(1, kids):
+                    kid = jnp.where(octant[0, other] == spot, other, kid)
+                fine = dot(theta_up[rows], wide[kid])
+                real, imag = fine[:, :LANES], fine[:, LANES:]
+                cos_part, sin_part = cos_sin(cosines[chunk][spot, rows])
+                cosines[chunk][spot, rows] = cos_part
+                sines[chunk][spot, rows] = sin_part
+                grid_sum[0, rows] += real * cos_part - imag * sin_part
+                grid_sum[1, rows] += real * sin_part + imag * cos_part
+                return inner
+
+            lax.fori_loop(0, kids, one_octant, 0)
+            for owner in range(samps):
+
+                @pl.when(part_of == owner // middle)
+                def _():
+                    for part in range(parts):
+                        outgoing[chunk][0, part, owner] = grid_sum[
+                            part, owner * theta_rows : (owner + 1) * theta_rows
+                        ]
+
+            @pl.when(turned == 0)
+            def _():
+                pl.semaphore_wait(barrier, samps - 1 + len(bits))
+
+            def one(step, inner):
+                peer = part_of * middle + step
+
+                @pl.when(peer != me)
+                def _():
+                    out_part(chunk, 0, peer).start()
+
+                return inner
+
+            lax.fori_loop(0, middle, one, 0)
+            return carry
+
+        def one_parent(parent, carry):
+            interpolate(parent)
             grid_sum[...] = jnp.zeros_like(grid_sum)
 
             if chunk > 0:
@@ -347,7 +406,7 @@
 
             if between:
 
-                @pl.when(parent == per_device // 2)
+                @pl.when(parent == min(1, per_device - 1))
                 def _():
                     run(between)
 
@@ -369,14 +428,20 @@
                     ]
             if chunk == 0:
 
-                @pl.when(parent == 0)
+                @pl.when(parent == per_device - 1)
                 def _():
-                    pl.semaphore_wait(barrier, samps - 1 + len(bits))
+                    for later in range(chunks):
+                        load(later).start()
 
                 send_out(chunk, parent)
             return carry
 
-        lax.fori_loop(0, per_device, one_parent, 0)
+        if chunk == 0:
+            interpolate(0)
+            grid_sum[...] = jnp.zeros_like(grid_sum)
+            load_angle(chunk).wait()
+            lax.fori_loop(0, 2, first_half, 0)
+        lax.fori_loop(1 if chunk == 0 else 0, per_device, one_parent, 0)
 
     def disaggregate(chunk, first, between):
         rows = slice(chunk * LANES, (chunk + 1) * LANES)
@@ -388,8 +453,8 @@
 
         def one_parent(parent, carry):
             returned_part(chunk, parent)
-            for function, *rest in between:
-                function(*rest, parent)
+            for function in between:
+                function(parent)
             for part in range(parts):
                 for owner in range(samps):
                     grid_sum[part, owner * theta_rows : (owner + 1) * theta_rows] = incoming[chunk][
@@ -453,21 +518,51 @@
                 for mask in [h + bit for h in held]:
                     await_bytes(sources[chunk].at[held_in(owner_of(mask), part)], box_recv.at[chunk, hop_slot(mask, part)])
 
-    def back_far_part(chunk, slot):
+    def back_far_part(chunk, slot, wanted=None):
         def one(step, carry):
-            back_part(chunk, slot, (1 - side) * middle + step).start()
-            return carry
-
-        @pl.when(outer)
-        def _():
-            lax.fori_loop(0, middle, one, 0)
+            peer = (1 - side) * middle + step
+
+            @pl.when(jnp.logical_or(wanted is None, at_rim(peer) == bool(wanted)))
+            def _():
+                back_part(chunk, slot, peer).start()
+
+            return carry
+
+        lax.fori_loop(0, middle, one, 0)
 
     def back_far(chunk):
         def one(slot, carry):
             back_far_part(chunk, slot)
             return carry
 
-        lax.fori_loop(0, per_device, one, 0)
+        @pl.when(outer)
+        def _():
+            lax.fori_loop(0, per_device, one, 0)
+
+    def back_last(parent):
+        def late(slot):
+            @pl.when(slot >= 0)
+            def _():
+                back_far_part(last, slot, False)
+
+        @pl.when(outer)
+        def _():
+            for lead in range(DELAY):
+
+                @pl.when(parent == 0)
+                def _():
+                    back_far_part(last, lead, True)
+
+            @pl.when(parent + DELAY < per_device)
+            def _():
+                back_far_part(last, parent + DELAY, True)
+
+            late(parent - DELAY)
+
+            @pl.when(parent == per_device - 1)
+            def _():
+                for lag in range(DELAY):
+                    late(per_device - DELAY + lag)
 
     def translate(chunk, between):
         await_bytes(sources[chunk].at[pl.ds(0, boxes // 2 * samps * per_device)], box_recv.at[chunk, 0])
@@ -499,36 +594,46 @@
 
                 there = lax.rem(me + step, samps)
 
-                @pl.when(jnp.logical_and(step > 0, jnp.logical_not(jnp.logical_and(outer, far(there)))))
+                distant = far(there)
+                late = jnp.logical_and(distant, jnp.logical_not(at_rim(there))) if chunk == last else False
+
+                @pl.when(jnp.logical_and(step > 0, jnp.logical_not(jnp.logical_or(jnp.logical_and(outer, distant), late))))
                 def _():
                     back_part(chunk, slot, there).start()
 
+                if chunk == last:
+
+                    @pl.when(jnp.logical_and(jnp.logical_and(late, slot >= DELAY), jnp.logical_not(outer)))
+                    def _():
+                        back_part(chunk, slot - DELAY, there).start()
+
                 return inner
 
             lax.fori_loop(0, samps, one, 0)
             return carry
 
         lax.fori_loop(0, per_device, receivers, 0)
+        if chunk == last:
+
+            @pl.when(jnp.logical_not(outer))
+            def _():
+                for slot in range(max(0, per_device - DELAY), per_device):
+                    back_far_part(chunk, slot, False)
 
     def returned_part(chunk, parent):
         await_bytes(incoming[chunk].at[parent, :, pl.ds(0, samps - 1)], back_recv.at[chunk * per_device + parent])
 
-    load_angle(0).start()
-    for parent in range(per_device):
-        load_child(parent).start()
     for copy in small:
         copy.start()
-    load_angle(0).wait()
-    turn(0)
+    load_child(0).start()
+    load_angle(0).start()
     for copy in small:
         copy.wait()
-    build_theta()
-    for parent in range(per_device):
-        load_child(parent).wait()
+    for parent in range(1, per_device):
+        load_child(parent).start()
     for chunk in range(1, chunks):
         load_angle(chunk).start()
-    for chunk in range(chunks):
-        load(chunk).start()
+    build_theta()
     called = {(send_far, 0)}
 
     def fresh(*calls):
@@ -549,16 +654,17 @@
             run(fresh((send_far, chunk - 1)))
         run(fresh((share, chunk - 2, 1)))
         aggregate(chunk, fresh((share, chunk - 1, 0), (pass_on, chunk - 2, 0)))
-    last = chunks - 1
     send_last(last)
     for chunk in range(chunks):
         if chunk == last:
-            run(fresh((send_far, last), (pass_on, last, 0), (share, last, 1), (back_far, last - 2)))
+            run(fresh((send_far, last), (share, last, 0), (share, last, 1), (back_far, last - 2), (pass_on, last, 0)))
         run(fresh((share, chunk, 0), (pass_on, chunk, 0)))
         run(fresh((share, chunk, 1), (pass_on, chunk, 1)))
         if chunk:
+            run(fresh((share, chunk + 1, 0)))
+        if chunk:
             back_keep(chunk - 1).start()
-        translate(chunk, fresh((share, chunk + 1, 1), (send_far, last), (share, last, 0)) if chunk + 1 < last else [])
+        translate(chunk, fresh((share, chunk + 1, 1), (send_far, last)) if chunk + 1 < last else [])
     for chunk in range(last):
         run(fresh((back_far, chunk)))
         if chunk + 1 < last:
@@ -566,7 +672,7 @@
         back_keep(chunk).wait()
         if chunk == 0:
             back_keep(last).start()
-        disaggregate(chunk, chunk == 0, [(back_far_part, last)] if chunk + 1 == last else [])
+        disaggregate(chunk, chunk == 0, [back_last] if chunk + 1 == last else [])
     if last == 0:
         run(fresh((back_far, last)))
         back_keep(last).start()

time: 118 us -> 115 us (0.975)
  Pallas kernels: 115 us -> 112 us
    pallas_call x1, Pallas kernels: 115 us -> 112 us  [local(): pl.pallas_call(functools.partial(step_kernel, boxes, samps, partners), ou...]
where the time goes in v4:
time: 115 us; the launch traced here: 114 us
  Pallas kernels  112 us (97%)
  local copies, waits for them, and re-layouts  2.19 us (2%)
    pallas_call x1, Pallas kernels, local(): pl.pallas_call(functools.partial(step_kernel, boxes, samps, partners), ou...  112 us

profile of v4, /device:TPU:0, one launch (start us, length us, event | category | flops | bytes accessed | tf_op | source)
XLA Modules:
  0.0 113.7 jit_solution(17562740656739586123)
XLA Ops:
  0.0 111.5 %shard_map.100 = f32[32,288,128]{2,1,0:T(8,128)S(1)} custom-call(s32[32,128]{1,0:T(8,128)} %bitcast.18, s32[32,128]{1,0:T(8,128)} %bitcast.19, s32[4,8]{1,0:T(4,128)} %octant_in.1, s32[4,192]{1,0:T(4,128)} %bitcast.22, f32[4,192]{1,0:T(4,128)} %bitcast.23, s32[4,384]{1,0:T(4,128)} %bitcast.20, f32[4,384]{1,0:T(4,128)} %bitcast.21, f32[32,288,128]{2,1,0:T(8,128)} %bitcast.17, ...), custom_call_target="tpu_custom_call" | custom-call | tf_op jit(solution)/shard_map/pallas_call | solution.py:723
  111.5 2.2 %copy.14 = f32[32,2,18432]{2,1,0:T(2,128)} copy(f32[32,2,18432]{2,1,0:T(2,128)S(1)} %bitcast.16) | data formatting | bytes 9437184

commit v5 on v4

--- a/solution.py
+++ b/solution.py
@@ -123,12 +123,6 @@
     def mate(bit):
         return group + bit - 2 * bit * lax.rem(lax.div(group, bit), 2)
 
-    barrier = pltpu.get_barrier_semaphore()
-    for step in range(1, samps):
-        pl.semaphore_signal(barrier, inc=1, device_id=(group, lax.rem(me + step, samps)), device_id_type=MESH)
-    for bit in bits:
-        pl.semaphore_signal(barrier, inc=1, device_id=(mate(bit), me), device_id_type=MESH)
-
     def load(chunk):
         return pltpu.make_async_copy(
             table.at[:, :, :, pl.ds(chunk * LANES, LANES)], operators[chunk], load_sem.at[chunk]
@@ -237,11 +231,11 @@
         pltpu.make_async_copy(source, place, small_sem.at[spot])
         for spot, (source, place) in enumerate(
             (
-                (octant_in, octant),
                 (theta_index_in, theta_index_t),
                 (theta_weight_in, theta_weight_t),
                 (phi_index_in, phi_index_t),
                 (phi_weight_in, phi_weight_t),
+                (octant_in, octant),
                 (src_in, src_rows),
                 (disp_in, disp_rows),
             )
@@ -368,7 +362,7 @@
                 grid_sum[1, rows] += real * sin_part + imag * cos_part
                 return inner
 
-            lax.fori_loop(0, kids, one_octant, 0)
+            lax.fori_loop(0, kids, one_octant, 0, unroll=8)
             for owner in range(samps):
 
                 @pl.when(part_of == owner // middle)
@@ -406,7 +400,7 @@
 
             if between:
 
-                @pl.when(parent == min(1, per_device - 1))
+                @pl.when(parent == per_device // 2)
                 def _():
                     run(between)
 
@@ -420,7 +414,7 @@
                 grid_sum[1] += real * sin_part + imag * cos_part
                 return inner
 
-            lax.fori_loop(0, kids, one_child, 0)
+            lax.fori_loop(0, kids, one_child, 0, unroll=8)
             for part in range(parts):
                 for owner in range(samps):
                     outgoing[chunk][parent, part, owner] = grid_sum[
@@ -480,7 +474,7 @@
                             ] = piece[parity * half : (parity + 1) * half, part * LANES : (part + 1) * LANES]
                 return inner
 
-            lax.fori_loop(0, kids, one_child, 0)
+            lax.fori_loop(0, kids, one_child, 0, unroll=8)
             ends = []
             for parity in range(2):
                 flat = wide_out[parity].reshape(kids * parts * half, 2 * LANES)
@@ -623,11 +617,18 @@
     def returned_part(chunk, parent):
         await_bytes(incoming[chunk].at[parent, :, pl.ds(0, samps - 1)], back_recv.at[chunk * per_device + parent])
 
-    for copy in small:
+    for copy in small[:5]:
         copy.start()
     load_child(0).start()
     load_angle(0).start()
-    for copy in small:
+    barrier = pltpu.get_barrier_semaphore()
+    for step in range(1, samps):
+        pl.semaphore_signal(barrier, inc=1, device_id=(group, lax.rem(me + step, samps)), device_id_type=MESH)
+    for bit in bits:
+        pl.semaphore_signal(barrier, inc=1, device_id=(mate(bit), me), device_id_type=MESH)
+    for copy in small[5:]:
+        copy.start()
+    for copy in small[:5]:
         copy.wait()
     for parent in range(1, per_device):
         load_child(parent).start()
@@ -650,11 +651,13 @@
         load_angle(chunk).wait()
         turn(chunk)
         send_last(chunk - 1)
+        run(fresh((share, chunk - 2, 1)))
         if chunk > 1:
             run(fresh((send_far, chunk - 1)))
-        run(fresh((share, chunk - 2, 1)))
         aggregate(chunk, fresh((share, chunk - 1, 0), (pass_on, chunk - 2, 0)))
     send_last(last)
+    for copy in small[5:]:
+        copy.wait()
     for chunk in range(chunks):
         if chunk == last:
             run(fresh((send_far, last), (share, last, 0), (share, last, 1), (back_far, last - 2), (pass_on, last, 0)))

time: 115 us -> 112 us (0.974)
  Pallas kernels: 112 us -> 109 us
    pallas_call x1, Pallas kernels: 112 us -> 109 us  [local(): pl.pallas_call(functools.partial(step_kernel, boxes, samps, partners), ou...]
where the time goes in v5:
time: 112 us
  Pallas kernels  109 us (97%)
  local copies, waits for them, and re-layouts  2.19 us (2%)
    pallas_call x1, Pallas kernels, local(): pl.pallas_call(functools.partial(step_kernel, boxes, samps, partners), ou...  109 us

profile of v5, /device:TPU:0, one launch (start us, length us, event | category | flops | bytes accessed | tf_op | source)
XLA Modules:
  0.0 111.5 jit_solution(4247009112975977370)
XLA Ops:
  0.0 109.3 %shard_map.100 = f32[32,288,128]{2,1,0:T(8,128)S(1)} custom-call(s32[32,128]{1,0:T(8,128)} %bitcast.18, s32[32,128]{1,0:T(8,128)} %bitcast.19, s32[4,8]{1,0:T(4,128)} %octant_in.1, s32[4,192]{1,0:T(4,128)} %bitcast.22, f32[4,192]{1,0:T(4,128)} %bitcast.23, s32[4,384]{1,0:T(4,128)} %bitcast.20, f32[4,384]{1,0:T(4,128)} %bitcast.21, f32[32,288,128]{2,1,0:T(8,128)} %bitcast.17, ...), custom_call_target="tpu_custom_call" | custom-call | tf_op jit(solution)/shard_map/pallas_call | solution.py:726
  109.3 2.2 %copy.14 = f32[32,2,18432]{2,1,0:T(2,128)} copy(f32[32,2,18432]{2,1,0:T(2,128)S(1)} %bitcast.16) | data formatting | bytes 9437184

commit v6 on v5

--- a/solution.py
+++ b/solution.py
@@ -11,7 +11,8 @@
 NP1 = 192
 LANES = 128
 MESH = pl.DeviceIdType.MESH
-DELAY = 1
+OUTER_LAG = 1
+INNER_LAG = 2
 VMEM_LIMIT = 56 * 1024 * 1024
 
 
@@ -38,23 +39,22 @@
     return lax.broadcasted_iota(jnp.int32, shape, axis)
 
 
-HALF_PI = (1.5703125, 4.837512969970703e-4, 7.54978995489188e-8)
+HALF_SINE = (0.5, -0.02083333395421505, 0.00026041659293696284, -1.5500672816415317e-06, 5.376032508053186e-09, -1.1664790661169988e-11)
+HALF_COSINE = (1.0, -0.125, 0.0026041646488010883, -2.1700563593185507e-05, 9.671927614363085e-08, -2.5440496931317114e-10)
+
+
+def series(square, terms):
+    total = terms[-1]
+    for term in terms[-2::-1]:
+        total = total * square + term
+    return total
 
 
 def cos_sin(angle):
-    turns = jnp.floor(angle * 0.6366197723675814 + 0.5)
-    rest = ((angle - turns * HALF_PI[0]) - turns * HALF_PI[1]) - turns * HALF_PI[2]
-    square = rest * rest
-    sine = -1.9515295891e-4 * square + 8.3321608736e-3
-    sine = (sine * square - 1.6666654611e-1) * square * rest + rest
-    cosine = 2.443315711809948e-5 * square - 1.388731625493765e-3
-    cosine = (cosine * square + 4.166664568298827e-2) * square * square - 0.5 * square + 1.0
-    half = jnp.floor(turns * 0.5)
-    odd = turns - 2.0 * half > 0.5
-    flip = half - 2.0 * jnp.floor(half * 0.5) > 0.5
-    sin_part = jnp.where(odd, cosine, sine)
-    cos_part = jnp.where(odd, -sine, cosine)
-    return jnp.where(flip, -cos_part, cos_part), jnp.where(flip, -sin_part, sin_part)
+    square = angle * angle
+    sine = series(square, HALF_SINE) * angle
+    twice = sine + sine
+    return 1.0 - twice * sine, twice * series(square, HALF_COSINE)
 
 
 def step_kernel(
@@ -173,12 +173,28 @@
             device_id_type=MESH,
         )
 
+    def whole_back(chunk):
+        return chunk == 0 and chunk < last
+
+    def back_slot(chunk, slot):
+        return 0 if whole_back(chunk) else chunk * per_device + slot
+
+    def back_copy(chunk, peer):
+        return pltpu.make_async_remote_copy(
+            src_ref=results[chunk].at[peer],
+            dst_ref=incoming[chunk].at[:, :, me],
+            send_sem=back_send.at[chunk],
+            recv_sem=back_recv.at[back_slot(chunk, 0)],
+            device_id=(group, peer),
+            device_id_type=MESH,
+        )
+
     def back_part(chunk, slot, peer):
         return pltpu.make_async_remote_copy(
             src_ref=results[chunk].at[peer, slot],
             dst_ref=incoming[chunk].at[slot, :, me],
             send_sem=back_send.at[chunk],
-            recv_sem=back_recv.at[chunk * per_device + slot],
+            recv_sem=back_recv.at[back_slot(chunk, slot)],
             device_id=(group, peer),
             device_id_type=MESH,
         )
@@ -290,27 +306,27 @@
         lax.fori_loop(1, middle, near_one, 0)
         if chunk == 0:
             lax.fori_loop(0, middle, far_one, 0)
-        else:
-
-            @pl.when(jnp.logical_not(outer))
-            def _():
-                lax.fori_loop(0, middle, far_one, 0)
+
+    def send_whole(chunk):
+        def one(step, carry):
+            out_copy(chunk, (1 - side) * middle + lax.rem(me - side * middle + 1 + step, middle)).start()
+            return carry
+
+        lax.fori_loop(0, middle, one, 0)
 
     def send_far(chunk):
-        def one(step, carry):
-            peer = lax.rem(me + step, samps)
-
-            @pl.when(jnp.logical_and(outer, far(peer)))
-            def _():
-                out_copy(chunk, peer).start()
-
-            return carry
-
-        lax.fori_loop(1, samps, one, 0)
+        @pl.when(outer)
+        def _():
+            send_whole(chunk)
 
     def send_last(chunk):
         if chunk > 0:
             send_out(chunk, per_device - 1)
+
+            @pl.when(jnp.logical_not(outer))
+            def _():
+                send_whole(chunk)
+
         keep(chunk).start()
 
     def aggregate(chunk, between):
@@ -529,9 +545,25 @@
             back_far_part(chunk, slot)
             return carry
 
+        def whole(step, carry):
+            back_copy(chunk, (1 - side) * middle + lax.rem(me - side * middle + 1 + step, middle)).start()
+            return carry
+
         @pl.when(outer)
         def _():
-            lax.fori_loop(0, per_device, one, 0)
+            if whole_back(chunk):
+                lax.fori_loop(0, middle, whole, 0)
+            else:
+                lax.fori_loop(0, per_device, one, 0)
+
+    def back_whole(chunk):
+        def whole(step, carry):
+            back_copy(chunk, (1 - side) * middle + lax.rem(me - side * middle + 1 + step, middle)).start()
+            return carry
+
+        @pl.when(jnp.logical_not(outer))
+        def _():
+            lax.fori_loop(0, middle, whole, 0)
 
     def back_last(parent):
         def late(slot):
@@ -541,22 +573,22 @@
 
         @pl.when(outer)
         def _():
-            for lead in range(DELAY):
+            for lead in range(OUTER_LAG):
 
                 @pl.when(parent == 0)
                 def _():
                     back_far_part(last, lead, True)
 
-            @pl.when(parent + DELAY < per_device)
+            @pl.when(parent + OUTER_LAG < per_device)
             def _():
-                back_far_part(last, parent + DELAY, True)
-
-            late(parent - DELAY)
+                back_far_part(last, parent + OUTER_LAG, True)
+
+            late(parent - OUTER_LAG)
 
             @pl.when(parent == per_device - 1)
             def _():
-                for lag in range(DELAY):
-                    late(per_device - DELAY + lag)
+                for lag in range(OUTER_LAG):
+                    late(per_device - OUTER_LAG + lag)
 
     def translate(chunk, between):
         await_bytes(sources[chunk].at[pl.ds(0, boxes // 2 * samps * per_device)], box_recv.at[chunk, 0])
@@ -591,15 +623,15 @@
                 distant = far(there)
                 late = jnp.logical_and(distant, jnp.logical_not(at_rim(there))) if chunk == last else False
 
-                @pl.when(jnp.logical_and(step > 0, jnp.logical_not(jnp.logical_or(jnp.logical_and(outer, distant), late))))
+                @pl.when(jnp.logical_and(step > 0, jnp.logical_not(distant if whole_back(chunk) else jnp.logical_or(jnp.logical_and(outer, distant), late))))
                 def _():
                     back_part(chunk, slot, there).start()
 
                 if chunk == last:
 
-                    @pl.when(jnp.logical_and(jnp.logical_and(late, slot >= DELAY), jnp.logical_not(outer)))
+                    @pl.when(jnp.logical_and(jnp.logical_and(late, slot >= INNER_LAG), jnp.logical_not(outer)))
                     def _():
-                        back_part(chunk, slot - DELAY, there).start()
+                        back_part(chunk, slot - INNER_LAG, there).start()
 
                 return inner
 
@@ -607,15 +639,18 @@
             return carry
 
         lax.fori_loop(0, per_device, receivers, 0)
+        if whole_back(chunk):
+            back_whole(chunk)
         if chunk == last:
 
             @pl.when(jnp.logical_not(outer))
             def _():
-                for slot in range(max(0, per_device - DELAY), per_device):
+                for slot in range(max(0, per_device - INNER_LAG), per_device):
                     back_far_part(chunk, slot, False)
 
     def returned_part(chunk, parent):
-        await_bytes(incoming[chunk].at[parent, :, pl.ds(0, samps - 1)], back_recv.at[chunk * per_device + parent])
+        if not whole_back(chunk):
+            await_bytes(incoming[chunk].at[parent, :, pl.ds(0, samps - 1)], back_recv.at[back_slot(chunk, parent)])
 
     for copy in small[:5]:
         copy.start()
@@ -673,6 +708,8 @@
         if chunk + 1 < last:
             run(fresh((back_far, chunk + 1)))
         back_keep(chunk).wait()
+        if whole_back(chunk):
+            await_bytes(incoming[chunk].at[:, :, pl.ds(0, samps - 1)], back_recv.at[back_slot(chunk, 0)])
         if chunk == 0:
             back_keep(last).start()
         disaggregate(chunk, chunk == 0, [back_last] if chunk + 1 == last else [])

time: 112 us -> 111 us (level)
    pallas_call x1, Pallas kernels: 109 us -> 108 us  [local(): pl.pallas_call(functools.partial(step_kernel, boxes, samps, partners), ou...]
where the time goes in v6:
time: 111 us; the launch traced here: 110 us
  Pallas kernels  108 us (97%)
  local copies, waits for them, and re-layouts  2.19 us (2%)
    pallas_call x1, Pallas kernels, local(): pl.pallas_call(functools.partial(step_kernel, boxes, samps, partners), ou...  108 us

profile of v6, /device:TPU:0, one launch (start us, length us, event | category | flops | bytes accessed | tf_op | source)
XLA Modules:
  0.0 110.3 jit_solution(10979305421398008539)
XLA Ops:
  0.0 108.1 %shard_map.100 = f32[32,288,128]{2,1,0:T(8,128)S(1)} custom-call(s32[32,128]{1,0:T(8,128)} %bitcast.18, s32[32,128]{1,0:T(8,128)} %bitcast.19, s32[4,8]{1,0:T(4,128)} %octant_in.1, s32[4,192]{1,0:T(4,128)} %bitcast.22, f32[4,192]{1,0:T(4,128)} %bitcast.23, s32[4,384]{1,0:T(4,128)} %bitcast.20, f32[4,384]{1,0:T(4,128)} %bitcast.21, f32[32,288,128]{2,1,0:T(8,128)} %bitcast.17, ...), custom_call_target="tpu_custom_call" | custom-call | tf_op jit(solution)/shard_map/pallas_call | solution.py:763
  108.1 2.2 %copy.14 = f32[32,2,18432]{2,1,0:T(2,128)} copy(f32[32,2,18432]{2,1,0:T(2,128)S(1)} %bitcast.16) | data formatting | bytes 9437184

commit v7 on v6

--- a/solution.py
+++ b/solution.py
@@ -12,7 +12,7 @@
 LANES = 128
 MESH = pl.DeviceIdType.MESH
 OUTER_LAG = 1
-INNER_LAG = 2
+INNER_LAG = 1
 VMEM_LIMIT = 56 * 1024 * 1024
 
 
@@ -174,10 +174,10 @@
         )
 
     def whole_back(chunk):
-        return chunk == 0 and chunk < last
+        return chunk < last
 
     def back_slot(chunk, slot):
-        return 0 if whole_back(chunk) else chunk * per_device + slot
+        return chunk if whole_back(chunk) else last + slot
 
     def back_copy(chunk, peer):
         return pltpu.make_async_remote_copy(
@@ -796,7 +796,7 @@
             dma((chunks, boxes - 1)),
             dma((chunks,)),
             dma((chunks,)),
-            dma((chunks * parents,)),
+            dma((chunks - 1 + parents,)),
             dma((7,)),
         ],
         compiler_params=pltpu.CompilerParams(

time: 111 us -> 111 us (level)
  no operation moved by 1% of the time
where the time goes in v7:
time: 111 us; the launch traced here: 110 us
  Pallas kernels  108 us (97%)
  local copies, waits for them, and re-layouts  2.19 us (2%)
    pallas_call x1, Pallas kernels, local(): pl.pallas_call(functools.partial(step_kernel, boxes, samps, partners), ou...  108 us

profile of v7, /device:TPU:0, one launch (start us, length us, event | category | flops | bytes accessed | tf_op | source)
XLA Modules:
  0.0 110.3 jit_solution(12831087418105377185)
XLA Ops:
  0.0 108.1 %shard_map.100 = f32[32,288,128]{2,1,0:T(8,128)S(1)} custom-call(s32[32,128]{1,0:T(8,128)} %bitcast.18, s32[32,128]{1,0:T(8,128)} %bitcast.19, s32[4,8]{1,0:T(4,128)} %octant_in.1, s32[4,192]{1,0:T(4,128)} %bitcast.22, f32[4,192]{1,0:T(4,128)} %bitcast.23, s32[4,384]{1,0:T(4,128)} %bitcast.20, f32[4,384]{1,0:T(4,128)} %bitcast.21, f32[32,288,128]{2,1,0:T(8,128)} %bitcast.17, ...), custom_call_target="tpu_custom_call" | custom-call | tf_op jit(solution)/shard_map/pallas_call | solution.py:763
  108.1 2.2 %copy.14 = f32[32,2,18432]{2,1,0:T(2,128)} copy(f32[32,2,18432]{2,1,0:T(2,128)S(1)} %bitcast.16) | data formatting | bytes 9437184
